TPU v7x, 32 devices: a whole 2x2x4 slice. The times are simulated.
32 devices in a mesh: frame: 8 (over y, x, core), tensor: 4 (over z).
Axes of the slice: x: 2, y: 2, z: 4, core: 2. Of those that a mesh axis runs over, the one named last changes fastest.
Arguments:
- hidden: bfloat16 [8192, 3072], P(('frame', 'tensor')), may hold values from -6 to 6
- qkv_weight: bfloat16 [3072, 3, 3072], P(None, None, 'tensor'), may hold values from -0.109375 to 0.109375
- norm_gain: float32 [2, 128], replicated, may hold values from 0.5 to 10, as said below
- out_grad: bfloat16 [8192, 3072], P('frame', 'tensor'), may hold values from -0.15625 to 0.15625
Outputs:
- attended: bfloat16 [8192, 3072], P('frame', 'tensor')
- weight_grad: float32 [3072, 3, 3072], P('frame', None, 'tensor')
Inputs may be any that keep to these rules, and one draw needn't show every extreme that they name: `norm_gain`: every gain is positive.
All inputs are finite; a program needn't handle non-finite values.
Results may differ from a plain program's by a relative error of at most 0.028.
The roundings to bfloat16 on the way count: a program that leaves them out, or rounds other values in their place, can miss the bound.
Values may be sent and summed in bfloat16 or wider, within the bound.
A program may use at most 192 MiB of HBM per device.

v0:
```python
import jax
import jax.numpy as jnp
from jax import lax
from jax.sharding import PartitionSpec as P

HEAD_DIM = 128


EPSILON = 1e-06


def padded(array, sides, width):
    for axis, dim in sides:
        size, length = (lax.axis_size(axis), array.shape[dim])
        up = [(i, (i + 1) % size) for i in range(size - 1)]
        down = [(j, i) for i, j in up]
        last = lax.slice_in_dim(array, length - width, length, axis=dim)
        initial = lax.slice_in_dim(array, 0, width, axis=dim)
        before = lax.ppermute(last, axis, up)
        after = lax.ppermute(initial, axis, down)
        array = jnp.concatenate([before, array, after], axis=dim)
    return array


def passed_along(value, axis, steps):
    count = lax.axis_size(axis)
    initial, last = (max(0, -steps), min(count, count - steps))
    return lax.ppermute(value, axis, [(source, source + steps) for source in range(initial, last)])


def norm_heads(projected, gain):
    inverse_rms = lax.rsqrt(jnp.mean(projected * projected, axis=-1, keepdims=True) + EPSILON)
    return (projected * inverse_rms * gain, inverse_rms)


def norm_back(projected, inverse_rms, gain, grad):
    weighted = grad * gain
    inner = jnp.mean(projected * weighted, axis=-1, keepdims=True)
    return inverse_rms * weighted - projected * (inverse_rms * inverse_rms * inverse_rms) * inner


def product(form, left, right):
    return jnp.einsum(form, left, right, preferred_element_type=jnp.float32)


def window_attention(query, window, out_grad, valid):
    total_rows = query.shape[0]
    block = min(512, total_rows)
    keys = window[:, 0]
    values = window[:, 1]
    factor = query.shape[-1] ** (-0.5)
    output_list = []
    query_grads = []
    keyval_grad = jnp.zeros(window.shape, jnp.float32)
    for first_row in range(0, total_rows, block):
        query_block = query[first_row : first_row + block]
        grad_block = out_grad[first_row : first_row + block]
        scores = product("qhd,khd->hqk", query_block, keys) * factor
        scores = jnp.where(valid[None, None, :], scores, -1e30)
        peak = jnp.max(scores, axis=-1, keepdims=True)
        raised = jnp.exp(scores - peak)
        weights = (raised / jnp.sum(raised, axis=-1, keepdims=True)).astype(jnp.bfloat16)
        attended = product("hqk,khd->qhd", weights, values).astype(jnp.bfloat16)
        row_dots = jnp.sum(grad_block.astype(jnp.float32) * attended.astype(jnp.float32), axis=-1)
        prob_grads = product("qhd,khd->hqk", grad_block, values)
        score_grads = (weights.astype(jnp.float32) * (prob_grads - row_dots.T[:, :, None])).astype(
            jnp.bfloat16
        )
        query_grad = product("hqk,khd->qhd", score_grads, keys) * factor
        key_grad = product("hqk,qhd->khd", score_grads, query_block) * factor
        value_grad = product("hqk,qhd->khd", weights, grad_block)
        keyval_grad = keyval_grad + jnp.stack([key_grad, value_grad], axis=1)
        output_list.append(attended)
        query_grads.append(query_grad)
    return (jnp.concatenate(output_list, 0), jnp.concatenate(query_grads, 0), keyval_grad)


def per_device(hidden, qkv_weight, norm_gain, out_grad):
    local = qkv_weight.shape[2]
    heads = local // HEAD_DIM
    gathered = lax.all_gather(hidden, "tensor", axis=0, tiled=True)
    projected = jnp.einsum("td,dkc->tkc", gathered, qkv_weight, preferred_element_type=jnp.float32)
    group_rows = projected.shape[0]
    half = group_rows // 2
    projected = projected.reshape(group_rows, 3, heads, HEAD_DIM)
    query_normed, query_rms = norm_heads(projected[:, 0], norm_gain[0])
    key_normed, key_rms = norm_heads(projected[:, 1], norm_gain[1])
    query = query_normed.astype(jnp.bfloat16)
    keyval = jnp.stack([key_normed.astype(jnp.bfloat16), projected[:, 2].astype(jnp.bfloat16)], 1)
    keyval = keyval.reshape(group_rows, 2, local)
    window = padded(keyval, (("frame", 0),), half)
    window = window.reshape(2 * group_rows, 2, heads, HEAD_DIM)
    group_index = lax.axis_index("frame")
    group_count = lax.axis_size("frame")
    place = group_index * group_rows + jnp.arange(2 * group_rows, dtype=jnp.int32)
    valid = (place >= half) & (place < group_count * group_rows + half)
    grads_heads = out_grad.reshape(group_rows, heads, HEAD_DIM)
    attended, query_grad, keyval_grad = window_attention(query, window, grads_heads, valid)
    query_raw_grad = norm_back(projected[:, 0], query_rms, norm_gain[0], query_grad)
    query_part = query_raw_grad.astype(jnp.bfloat16).reshape(group_rows, 1, local)

    def weight_term(grads):
        return jnp.einsum("td,tkc->dkc", gathered, grads, preferred_element_type=jnp.float32)

    query_weight = lax.psum_scatter(
        weight_term(query_part).astype(jnp.bfloat16), "frame", scatter_dimension=0, tiled=True
    ).astype(jnp.float32)
    keyval_grad = keyval_grad.reshape(2 * group_rows, 2, local)
    lower = keyval_grad[:half]
    own = keyval_grad[half : half + group_rows]
    upper = keyval_grad[half + group_rows :]
    from_next = passed_along(lower.astype(jnp.bfloat16), "frame", -1).astype(lower.dtype)
    from_prev = passed_along(upper.astype(jnp.bfloat16), "frame", 1).astype(upper.dtype)
    keyval_grad = (own + jnp.concatenate([from_prev, from_next], 0)).reshape(
        group_rows, 2, heads, HEAD_DIM
    )
    key_raw_grad = norm_back(projected[:, 1], key_rms, norm_gain[1], keyval_grad[:, 0])
    keyval_part = jnp.stack(
        [key_raw_grad.astype(jnp.bfloat16), keyval_grad[:, 1].astype(jnp.bfloat16)], 1
    )
    keyval_part = keyval_part.reshape(group_rows, 2, local)
    keyval_weight = lax.psum_scatter(
        weight_term(keyval_part).astype(jnp.bfloat16), "frame", scatter_dimension=0, tiled=True
    ).astype(jnp.float32)
    weight_grad = jnp.concatenate([query_weight, keyval_weight], 1)
    return (attended.reshape(group_rows, local), weight_grad)


def solution(mesh):
    placed = (P(("frame", "tensor"), None), P(None, None, "tensor"), P(), P("frame", "tensor"))
    return jax.shard_map(
        per_device,
        mesh=mesh,
        in_specs=placed,
        out_specs=(P("frame", "tensor"), P("frame", None, "tensor")),
        check_vma=False,
    )
```

profile of v0, /device:TPU:0, one launch (start us, length us, event | category | flops | bytes accessed | tf_op | source)
XLA Modules:
  0.0 555.3 jit_solution(2576187574659647827)
XLA Ops:
  8.7 118.9 %all-gather.2.cloned.1.call-done = bf16[1024,3072]{1,0:T(8,128)(2,1)} async-done(((bf16[256,3072]{1,0:T(8,128)(2,1)}), bf16[1024,3072]{1,0:T(8,128)(2,1)}) %all-gather.2.cloned.1.call-update) | async-done | bytes 6291472 | tf_op jit(solution)/shard_map/all_gather | solution.py:81
  127.6 19.6 %fusion.13 = f32[1024,3,768]{0,2,1:T(8,128)S(1)} fusion(bf16[3072,3,768]{2,0,1:T(8,128)(2,1)} %param.5, bf16[1024,3072]{1,0:T(8,128)(2,1)} %all-gather.2.cloned.1.call-done), kind=kOutput, calls=%fused_computation.25 | convolution fusion | flops 14495514624 | bytes 29884416 | tf_op jit(solution)/shard_map/td,dkc->tkc/dot_general | solution.py:82
  147.9 1.1 multiply_multiply_fusion
  148.9 3.2 fusion.62
  152.2 2.1 fusion.36
  154.3 1.3 collective-permute-start.1
  155.6 4.6 collective-permute-start
  160.4 1.2 copy.53
  161.5 1.2 copy.60
  162.7 2.4 copy.93
  166.0 1.9 fusion.28
  168.4 5.0 pad_maximum_fusion
  173.4 14.0 %fusion.65 = (f32[6,512]{1,0:T(8,128)S(1)}, f32[6,512,2048]{2,1,0:T(8,128)}) fusion(pred[2048]{0:T(1024)(128)(4,1)S(1)} %fusion.55, bf16[2048,2,6,128]{0,3,2,1:T(8,128)(2,1)} %bitcast.169, bf16[1024,6,128]{2,0,1:T(8,128)(2,1)} %fusion.28), kind=kOutput, calls=%fused_computation.109 | convolution fusion | flops 1635780608 | bytes 29112320 | tf_op jit(solution)/shard_map/sub | solution.py:61
  187.4 14.2 %divide_convert_fusion = bf16[6,512,2048]{2,1,0:T(8,128)(2,1)} fusion(f32[6,512,2048]{2,1,0:T(8,128)} %get-tuple-element.25, f32[6,512]{1,0:T(8,128)S(1)} %get-tuple-element.24), kind=kLoop, calls=%fused_computation.6 | loop fusion | flops 12582912 | bytes 37761024 | tf_op jit(solution)/shard_map/convert_element_type | solution.py:62
  201.7 10.8 %multiply_reduce_fusion = (f32[512,6]{0,1:T(8,128)S(1)}, bf16[512,6,128]{0,2,1:T(8,128)(2,1)}) fusion(bf16[512,6,128]{0,2,1:T(8,128)(2,1)S(1)} %bitcast.194, bf16[6,512,2048]{2,1,0:T(8,128)(2,1)} %divide_convert_fusion, bf16[2048,2,6,128]{0,3,2,1:T(8,128)(2,1)} %bitcast.170), kind=kOutput, calls=%fused_computation.72 | convolution fusion | flops 1612575744 | bytes 17313792 | tf_op jit(solution)/shard_map/hqk,khd->qhd/dot_general | solution.py:43
  212.5 9.0 %convolution_bitcast_fusion = f32[2048,1,6,128]{0,3,2,1:T(8,128)} fusion(bf16[512,6,128]{0,2,1:T(8,128)(2,1)S(1)} %bitcast.195, bf16[6,512,2048]{2,1,0:T(8,128)(2,1)} %divide_convert_fusion), kind=kOutput, calls=%fused_computation.31 | convolution fusion | flops 1610612736 | bytes 19660800 | tf_op jit(solution)/shard_map/hqk,qhd->khd/dot_general | solution.py:43
  221.5 10.7 %fusion.2 = bf16[6,512,2048]{2,1,0:T(8,128)(2,1)} fusion(bf16[6,512,2048]{2,1,0:T(8,128)(2,1)} %divide_convert_fusion, f32[6,512]{1,0:T(8,128)S(1)} %bitcast.208, bf16[512,6,128]{0,2,1:T(8,128)(2,1)} %bitcast.193, bf16[2048,2,6,128]{0,3,2,1:T(8,128)(2,1)} %bitcast.171), kind=kOutput, calls=%fused_computation.3 | convolution fusion | flops 1635778560 | bytes 29110272 | tf_op jit(solution)/shard_map/qhd,khd->hqk/dot_general | solution.py:43
  232.2 10.2 %multiply_bitcast_fusion.2 = f32[512,6,128]{2,0,1:T(8,128)} fusion(bf16[6,512,2048]{2,1,0:T(8,128)(2,1)} %fusion.2, bf16[2048,2,6,128]{0,3,2,1:T(8,128)(2,1)} %bitcast.172), kind=kOutput, calls=%fused_computation.71 | convolution fusion | flops 1611005952 | bytes 17301504 | tf_op jit(solution)/shard_map/hqk,khd->qhd/dot_general | solution.py:43
  242.4 4.7 multiply_bitcast_fusion
  247.1 14.0 %fusion.70 = (f32[6,512]{1,0:T(8,128)S(1)}, f32[6,512,2048]{2,1,0:T(8,128)}) fusion(pred[2048]{0:T(1024)(128)(4,1)S(1)} %fusion.55, bf16[2048,2,6,128]{0,3,2,1:T(8,128)(2,1)} %bitcast.173, bf16[1024,6,128]{2,0,1:T(8,128)(2,1)} %fusion.28), kind=kOutput, calls=%fused_computation.110 | convolution fusion | flops 1635780608 | bytes 29112320 | tf_op jit(solution)/shard_map/sub | solution.py:61
  261.1 3.1 copy.66
  264.2 14.5 %divide_convert_fusion.1 = bf16[6,512,2048]{2,1,0:T(8,128)(2,1)} fusion(f32[6,512,2048]{2,1,0:T(8,128)} %get-tuple-element.27, f32[6,512]{1,0:T(8,128)S(1)} %get-tuple-element.26), kind=kLoop, calls=%fused_computation.9 | loop fusion | flops 12582912 | bytes 37761024 | tf_op jit(solution)/shard_map/convert_element_type | solution.py:62
  278.8 10.7 %multiply_reduce_fusion.1 = (f32[512,6]{0,1:T(8,128)S(1)}, bf16[512,6,128]{0,2,1:T(8,128)(2,1)}) fusion(bf16[512,6,128]{0,2,1:T(8,128)(2,1)S(1)} %bitcast.191, bf16[6,512,2048]{2,1,0:T(8,128)(2,1)} %divide_convert_fusion.1, bf16[2048,2,6,128]{0,3,2,1:T(8,128)(2,1)} %bitcast.174), kind=kOutput, calls=%fused_computation.74 | convolution fusion | flops 1612575744 | bytes 17313792 | tf_op jit(solution)/shard_map/hqk,khd->qhd/dot_general | solution.py:43
  289.5 10.6 %fusion.3 = bf16[6,512,2048]{2,1,0:T(8,128)(2,1)} fusion(bf16[6,512,2048]{2,1,0:T(8,128)(2,1)} %divide_convert_fusion.1, f32[6,512]{1,0:T(8,128)S(1)} %bitcast.209, bf16[512,6,128]{0,2,1:T(8,128)(2,1)} %bitcast.190, bf16[2048,2,6,128]{0,3,2,1:T(8,128)(2,1)} %bitcast.175), kind=kOutput, calls=%fused_computation.5 | convolution fusion | flops 1635778560 | bytes 29110272 | tf_op jit(solution)/shard_map/qhd,khd->hqk/dot_general | solution.py:43
  300.1 7.4 %multiply_bitcast_fusion.3 = f32[512,6,128]{2,0,1:T(8,128)S(1)} fusion(bf16[6,512,2048]{2,1,0:T(8,128)(2,1)} %fusion.3, bf16[2048,2,6,128]{0,3,2,1:T(8,128)(2,1)} %bitcast.176), kind=kOutput, calls=%fused_computation.73 | convolution fusion | flops 1611005952 | bytes 17301504 | tf_op jit(solution)/shard_map/hqk,khd->qhd/dot_general | solution.py:43
  307.5 1.1 copy-done.13
  309.6 3.2 copy.59
  312.8 2.5 fusion.18
  315.3 9.4 %fusion.15 = bf16[3072,768]{0,1:T(8,128)(2,1)} fusion(bf16[1024,768]{0,1:T(8,128)(2,1)S(1)} %fusion.18, bf16[1024,3072]{1,0:T(8,128)(2,1)} %all-gather.2.cloned.1.call-done), kind=kOutput, calls=%fused_computation.30 | convolution fusion | flops 4834197504 | bytes 12582912 | tf_op jit(solution)/shard_map/td,tkc->dkc/dot_general | solution.py:103
  324.7 6.6 %copy.89 = bf16[3072,768]{1,0:T(8,128)(2,1)} copy(bf16[3072,768]{0,1:T(8,128)(2,1)} %fusion.15) | data formatting | bytes 9437184
  332.5 6.5 %convolution_bitcast_fusion.1 = f32[2048,1,6,128]{0,3,2,1:T(8,128)S(1)} fusion(bf16[512,6,128]{0,2,1:T(8,128)(2,1)S(1)} %bitcast.192, bf16[6,512,2048]{2,1,0:T(8,128)(2,1)} %divide_convert_fusion.1), kind=kOutput, calls=%fused_computation.32 | convolution fusion | flops 1610612736 | bytes 19660800 | tf_op jit(solution)/shard_map/hqk,qhd->khd/dot_general | solution.py:43
  339.1 6.8 %multiply_bitcast_fusion.1 = f32[2048,1,6,128]{0,3,2,1:T(8,128)S(1)} fusion(bf16[6,512,2048]{2,1,0:T(8,128)(2,1)} %fusion.3, bf16[1024,6,128]{2,0,1:T(8,128)(2,1)S(1)} %copy-done.11), kind=kOutput, calls=%fused_computation.28 | convolution fusion | flops 1612185600 | bytes 19660800 | tf_op jit(solution)/shard_map/hqk,qhd->khd/dot_general | solution.py:43
  345.9 8.1 %fusion.61 = (bf16[2048,2,6,128]{0,3,2,1:T(8,128)(2,1)}, f32[2048,2,6,128]{0,3,2,1:T(8,128)}) fusion(f32[2048,1,6,128]{0,3,2,1:T(8,128)S(1)} %bitcast.185, f32[2048,1,6,128]{0,3,2,1:T(8,128)S(1)} %bitcast.187, f32[2048,1,6,128]{0,3,2,1:T(8,128)S(1)} %convolution_bitcast_fusion.1, f32[2048,1,6,128]{0,3,2,1:T(8,128)S(1)} %multiply_bitcast_fusion.1), kind=kLoop, calls=%fused_computation.105 | loop fusion | flops 12582912 | bytes 44040192 | tf_op jit(solution)/shard_map/convert.6
  354.0 2.3 fusion.63
  356.3 1.3 collective-permute-start.3
  357.6 25.6 %collective-permute-start.2 = (bf16[512,2,768]{0,2,1:T(8,128)(2,1)S(1)}, bf16[512,2,768]{0,2,1:T(8,128)(2,1)S(1)}, u32[]{:S(2)}, u32[]{:S(2)}) collective-permute-start(bf16[512,2,768]{0,2,1:T(8,128)(2,1)S(1)} %bitcast.203), channel_id=1, source_target_pairs={{0,4},{4,8},{8,12},{12,16},{16,20},{20,24},{24,28},{1,5},{5,9},{9,... | collective-permute-start | bytes 4718600 | tf_op jit(solution)/shard_map/ppermute | solution.py:28
  384.1 2.1 collective-permute-done.2
  386.2 4.2 slice_add_fusion
  394.3 12.2 %convolution_convert_fusion = bf16[2,768,3072]{2,1,0:T(8,128)(2,1)} fusion(bf16[1024,3072]{1,0:T(8,128)(2,1)S(1)} %bitcast.211, bf16[1024,1,768]{0,2,1:T(8,128)(2,1)S(1)} %bitcast.202, bf16[1024,1,768]{0,2,1:T(8,128)(2,1)S(1)} %bitcast.205), kind=kOutput, calls=%fused_computation.21 | convolution fusion | flops 9669967872 | bytes 18874368 | tf_op jit(solution)/shard_map/td,tkc->dkc/dot_general | solution.py:103
  406.5 12.7 %copy.91 = bf16[3072,1536]{1,0:T(8,128)(2,1)} copy(bf16[3072,1536]{0,1:T(8,128)(2,1)} %bitcast.196) | data formatting | bytes 18874368
  419.2 1.1 copy-done.15
  420.7 1.6 copy.70
  422.3 1.5 reduce-scatter.7.cloned.1.call-done
  423.8 2.1 copy.90
  425.9 115.7 %reduce-scatter.9.cloned.1.call-done = bf16[384,1536]{1,0:T(8,128)(2,1)} async-done(((bf16[3072,1536]{1,0:T(8,128)(2,1)}), bf16[384,1536]{1,0:T(8,128)(2,1)}) %reduce-scatter.9.cloned.1.call-update) | async-done | bytes 1179664
  541.7 2.4 copy.92
  544.0 1.6 maximum_convert_fusion
  545.7 2.9 copy.71
  (88 shorter events, 11.0 us)
Async XLA Ops:
  7.2 120.5 %all-gather.2.cloned.1.call-start = ((), (), s32[]{:S(2)}) async-start(), calls=%async_computation.2 | async-start | bytes 7864320 | tf_op jit(solution)/shard_map/all_gather | solution.py:81
  7.9 415.9 %reduce-scatter.7.cloned.1.call-start = ((), (), s32[]{:S(2)}) async-start(), calls=%async_computation.3 | async-start | bytes 5308416
  8.7 140.2 %copy-start.20 = (f32[128]{0:T(128)}, f32[128]{0:T(128)S(1)}, u32[]{:S(2)}) copy-start(f32[128]{0:T(128)S(1)} %get-tuple-element.23) | copy-start | bytes 1540
  147.2 7.0 %copy-start.1 = (f32[1024,3,768]{0,2,1:T(8,128)}, f32[1024,3,768]{0,2,1:T(8,128)S(1)}, u32[]{:S(2)}) copy-start(f32[1024,3,768]{0,2,1:T(8,128)S(1)} %fusion.13) | copy-start | bytes 28311556
  147.9 4.3 copy-start.3
  148.9 3.2 copy-start.17
  152.1 2.2 copy-start.5
  152.1 8.1 %copy-start.14 = (bf16[1024,768]{1,0:T(8,128)(2,1)S(1)}, bf16[1024,768]{1,0:T(8,128)(2,1)}, u32[]{:S(2)}) copy-start(bf16[1024,768]{1,0:T(8,128)(2,1)} %param.7) | copy-start | bytes 4718596
  154.3 13.6 %collective-permute-start.1 = (bf16[512,2,768]{0,2,1:T(8,128)(2,1)}, bf16[512,2,768]{0,2,1:T(8,128)(2,1)}, u32[]{:S(2)}, u32[]{:S(2)}) collective-permute-start(bf16[512,2,768]{0,2,1:T(8,128)(2,1)} %bitcast.7), channel_id=1, source_target_pairs={{4,0},{8,4},{12,8},{16,12},{20,16},{24,20},{28,24},{5,1},{9,5},{13... | collective-permute-start | bytes 4718600 | tf_op jit(solution)/shard_map/ppermute | solution.py:20
  155.6 12.3 %collective-permute-start = (bf16[512,2,768]{0,2,1:T(8,128)(2,1)}, bf16[512,2,768]{0,2,1:T(8,128)(2,1)}, u32[]{:S(2)}, u32[]{:S(2)}) collective-permute-start(bf16[512,2,768]{0,2,1:T(8,128)(2,1)} %bitcast.4), channel_id=1, source_target_pairs={{0,4},{4,8},{8,12},{12,16},{16,20},{20,24},{24,28},{1,5},{5,9},{9,... | collective-permute-start | bytes 4718600 | tf_op jit(solution)/shard_map/ppermute | solution.py:19
  166.0 1.9 copy-start.4
  166.0 2.4 copy-start.6
  187.4 14.2 %copy-start.9 = (bf16[512,768]{0,1:T(8,128)(2,1)S(1)}, bf16[512,768]{0,1:T(8,128)(2,1)}, u32[]{:S(2)}) copy-start(bf16[512,768]{0,1:T(8,128)(2,1)} %copy.60) | copy-start | bytes 2359300
  232.2 10.2 %copy-start = (bf16[6,512,2048]{2,1,0:T(8,128)(2,1)S(1)}, bf16[6,512,2048]{2,1,0:T(8,128)(2,1)}, u32[]{:S(2)}) copy-start(bf16[6,512,2048]{2,1,0:T(8,128)(2,1)} %fusion.2) | copy-start | bytes 37748740
  232.2 10.2 %copy-start.10 = (bf16[1024,6,128]{2,0,1:T(8,128)(2,1)S(1)}, bf16[1024,6,128]{2,0,1:T(8,128)(2,1)}, u32[]{:S(2)}) copy-start(bf16[1024,6,128]{2,0,1:T(8,128)(2,1)} %fusion.28) | copy-start | bytes 4718596
  264.2 14.5 %copy-start.7 = (bf16[512,768]{0,1:T(8,128)(2,1)S(1)}, bf16[512,768]{0,1:T(8,128)(2,1)}, u32[]{:S(2)}) copy-start(bf16[512,768]{0,1:T(8,128)(2,1)} %copy.53) | copy-start | bytes 2359300
  300.1 8.6 %copy-start.12 = (f32[512,6,128]{2,0,1:T(8,128)S(1)}, f32[512,6,128]{2,0,1:T(8,128)}, u32[]{:S(2)}) copy-start(f32[512,6,128]{2,0,1:T(8,128)} %multiply_bitcast_fusion.2) | copy-start | bytes 4718596
  307.5 1.1 copy-start.13
  309.6 3.2 copy-start.2
  331.4 1.1 copy-start.8
  331.4 7.6 %copy-start.11 = (bf16[1024,6,128]{2,0,1:T(8,128)(2,1)S(1)}, bf16[1024,6,128]{2,0,1:T(8,128)(2,1)}, u32[]{:S(2)}) copy-start(bf16[1024,6,128]{2,0,1:T(8,128)(2,1)} %fusion.28) | copy-start | bytes 4718596
  331.4 210.3 %reduce-scatter.9.cloned.1.call-start = ((), (), s32[]{:S(2)}) async-start(), calls=%async_computation.4 | async-start | bytes 10616832
  332.5 13.4 %slice-start.3 = ((s8[6291456]{0:T(1024)(128)(4,1)}), s8[4194304]{0:T(1024)(128)(4,1)S(1)}, s32[]{:S(2)}) async-start(s8[6291456]{0:T(1024)(128)(4,1)} %bitcast.184), calls=%async_computation.8 | async-start | bytes 8388608
  332.5 13.4 %slice-start.5 = ((s8[6291456]{0:T(1024)(128)(4,1)}), s8[4194304]{0:T(1024)(128)(4,1)S(1)}, s32[]{:S(2)}) async-start(s8[6291456]{0:T(1024)(128)(4,1)} %bitcast.186), calls=%async_computation.10 | async-start | bytes 8388608
  339.0 6.8 %slice-start.4 = ((s8[6291456]{0:T(1024)(128)(4,1)}), s8[2097152]{0:T(1024)(128)(4,1)S(1)}, s32[]{:S(2)}) async-start(s8[6291456]{0:T(1024)(128)(4,1)} %bitcast.184), calls=%async_computation.9 | async-start | bytes 4194304
  339.1 6.8 %slice-start.6 = ((s8[6291456]{0:T(1024)(128)(4,1)}), s8[2097152]{0:T(1024)(128)(4,1)S(1)}, s32[]{:S(2)}) async-start(s8[6291456]{0:T(1024)(128)(4,1)} %bitcast.186), calls=%async_computation.11 | async-start | bytes 4194304
  354.0 36.6 %slice-start = ((s8[9437184]{0:T(1024)(128)(4,1)}), s8[4194304]{0:T(1024)(128)(4,1)S(1)}, s32[]{:S(2)}) async-start(s8[9437184]{0:T(1024)(128)(4,1)} %bitcast.180), calls=%async_computation.5 | async-start | bytes 8388608
  356.3 27.8 %collective-permute-start.3 = (bf16[512,2,768]{0,2,1:T(8,128)(2,1)S(1)}, bf16[512,2,768]{0,2,1:T(8,128)(2,1)S(1)}, u32[]{:S(2)}, u32[]{:S(2)}) collective-permute-start(bf16[512,2,768]{0,2,1:T(8,128)(2,1)S(1)} %bitcast.204), channel_id=1, source_target_pairs={{4,0},{8,4},{12,8},{16,12},{20,16},{24,20},{28,24},{5,1},{9,5},{13... | collective-permute-start | bytes 4718600 | tf_op jit(solution)/shard_map/ppermute | solution.py:28
  357.6 28.6 %collective-permute-start.2 = (bf16[512,2,768]{0,2,1:T(8,128)(2,1)S(1)}, bf16[512,2,768]{0,2,1:T(8,128)(2,1)S(1)}, u32[]{:S(2)}, u32[]{:S(2)}) collective-permute-start(bf16[512,2,768]{0,2,1:T(8,128)(2,1)S(1)} %bitcast.203), channel_id=1, source_target_pairs={{0,4},{4,8},{8,12},{12,16},{16,20},{20,24},{24,28},{1,5},{5,9},{9,... | collective-permute-start | bytes 4718600 | tf_op jit(solution)/shard_map/ppermute | solution.py:28
  386.2 4.5 slice-start.1
  386.2 4.5 slice-start.2
  390.4 0.7 copy-start.21
  391.1 0.9 copy-start.18
  391.1 0.9 copy-start.19
  391.1 2.3 slice-start.7
  392.0 2.3 slice-start.8
  419.2 1.1 copy-start.15
  419.2 1.4 copy-start.16
Sparse Core Ops, SparseCore 0:
  9.5 118.0 all-gather.1
  331.5 92.2 reduce-scatter.6
  427.3 114.2 reduce-scatter.8
where the time goes:
time: 562 us; the launch traced here: 555 us
  waiting for transfers between devices  240 us (43%)
  matrix products  157 us (28%)
  other arithmetic  62.7 us (11%)
  local copies, waits for them, and re-layouts  48.6 us (9%)
  starting transfers between devices  33.2 us (6%)
  between operations  14.4 us (3%)
    all_gather x1, waiting for transfers between devices, per_device(): gathered = lax.all_gather(hidden, 'tensor', axis=0, tiled=True)  119 us
    unnamed x5, waiting for transfers between devices  118 us
    dot_general x10, matrix products, product(): return jnp.einsum(form, left, right, preferred_element_type=jnp.float32)  87.5 us
    unnamed x69, local copies, waits for them, and re-layouts  36.4 us
    convert_element_type x2, other arithmetic, window_attention(): (raised / jnp.sum(raised, axis=-1, keepdims=True)).astype(jnp.bfloat16)  28.8 us
    sub x2, matrix products, window_attention(): raised = jnp.exp(scores - peak)  28.1 us
    ppermute x2, starting transfers between devices, passed_along(): lax.ppermute(value, axis, [(source, source + steps) for source in range(i...  26.9 us
    dot_general x2, matrix products, weight_term(): jnp.einsum('td,tkc->dkc', gathered, grads, preferred_element_type=jnp.flo...  21.6 us
  transfers between devices with their start and end apart: 7, of which 5 were waited for; matrix products, arithmetic and copies ran while one was open for 12% of the time, Pallas kernels for 0%

commit v1 on v0

v1 whole, which is shorter than its diff:
```python
import functools
import math

import jax
import jax.numpy as jnp
from jax import lax
from jax.experimental import pallas as pl
from jax.experimental.pallas import tpu as pltpu
from jax.sharding import PartitionSpec as P

HEAD_DIM = 128
EPSILON = 1e-06
MASKED = -1e30
NT = (((1,), (1,)), ((), ()))


def ppermute_by(value, axis, steps):
    count = lax.axis_size(axis)
    initial, last = (max(0, -steps), min(count, count - steps))
    return lax.ppermute(value, axis, [(source, source + steps) for source in range(initial, last)])


def inverse_rms_of(raw):
    return lax.rsqrt(jnp.mean(raw * raw, axis=-1, keepdims=True) + EPSILON)


def norm_back(raw, inverse_rms, gain, grad):
    weighted = grad * gain
    inner = jnp.mean(raw * weighted, axis=-1, keepdims=True)
    return inverse_rms * weighted - raw * (inverse_rms * inverse_rms * inverse_rms) * inner


def dot32(left, right):
    return jnp.dot(left, right, preferred_element_type=jnp.float32)


def dot_nt(left, right):
    return lax.dot_general(left, right, NT, preferred_element_type=jnp.float32)


def key_norm_kernel(raw_ref, gain_ref, out_ref):
    raw = raw_ref[...]
    out_ref[...] = (raw * inverse_rms_of(raw) * gain_ref[1:2]).astype(out_ref.dtype)


def key_norm(raw, gain):
    rows, local = raw.shape
    spec = pl.BlockSpec((rows, HEAD_DIM), lambda h: (0, h))
    return pl.pallas_call(
        key_norm_kernel,
        grid=(local // HEAD_DIM,),
        in_specs=[spec, pl.BlockSpec(gain.shape, lambda h: (0, 0))],
        out_specs=spec,
        out_shape=jax.ShapeDtypeStruct(raw.shape, jnp.bfloat16),
        name="key_norm",
    )(raw, gain)


def key_back_kernel(dk_ref, dv_ref, pk_ref, pv_ref, nk_ref, nv_ref, raw_ref, gain_ref, kout_ref, vout_ref):
    half = pk_ref.shape[0]
    gain = gain_ref[1:2]
    for part, (k_edge, v_edge) in enumerate(((pk_ref, pv_ref), (nk_ref, nv_ref))):
        rows = pl.ds(part * half, half)
        raw = raw_ref[rows]
        grad = dk_ref[rows] + k_edge[...].astype(jnp.float32)
        kout_ref[rows] = norm_back(raw, inverse_rms_of(raw), gain, grad).astype(jnp.bfloat16)
        vout_ref[rows] = (dv_ref[rows] + v_edge[...].astype(jnp.float32)).astype(jnp.bfloat16)


def key_back(dk, dv, pk, pv, nk, nv, raw, gain):
    rows, local = dk.shape
    spec = pl.BlockSpec((rows, HEAD_DIM), lambda h: (0, h))
    edge = pl.BlockSpec((pk.shape[0], HEAD_DIM), lambda h: (0, h))
    shape = jax.ShapeDtypeStruct(dk.shape, jnp.bfloat16)
    return pl.pallas_call(
        key_back_kernel,
        grid=(local // HEAD_DIM,),
        in_specs=[spec, spec, edge, edge, edge, edge, spec, pl.BlockSpec(gain.shape, lambda h: (0, 0))],
        out_specs=(spec, spec),
        out_shape=(shape, shape),
        name="key_back",
    )(dk, dv, pk, pv, nk, nv, raw, gain)


def attend_kernel(
    bias_ref, gain_ref, raw_ref, grad_ref, kp_ref, ko_ref, kn_ref, vp_ref, vo_ref, vn_ref,
    att_ref, qpart_ref, dk_ref, dv_ref, dkp_ref, dvp_ref, dkn_ref, dvn_ref,
    kt, vt, score, prob_grad, weight, score_grad, dk_acc, dv_acc,
):
    half = kp_ref.shape[0]
    total = dk_acc.shape[0]
    step, last = pl.program_id(1), pl.num_programs(1) - 1
    factor = HEAD_DIM ** (-0.5)
    chunks = [
        (kp_ref, vp_ref, slice(0, half), bias_ref[0]),
        (ko_ref, vo_ref, slice(0, half), None),
        (ko_ref, vo_ref, slice(half, 2 * half), None),
        (kn_ref, vn_ref, slice(0, half), bias_ref[1]),
    ]

    @pl.when(step == 0)
    def _():
        for i, (k_ref, v_ref, rows, _) in enumerate(chunks):
            kt[:, i * half : (i + 1) * half] = k_ref[rows].T
            vt[:, i * half : (i + 1) * half] = v_ref[rows].T
        dk_acc[...] = jnp.zeros_like(dk_acc)
        dv_acc[...] = jnp.zeros_like(dv_acc)

    raw = raw_ref[...]
    gain = gain_ref[0:1]
    inverse_rms = inverse_rms_of(raw)
    query = (raw * inverse_rms * gain).astype(jnp.bfloat16)
    grad = grad_ref[...]
    peak = None
    for i, (k_ref, v_ref, rows, bias) in enumerate(chunks):
        place = slice(i * half, (i + 1) * half)
        s = dot_nt(k_ref[rows], query)
        if bias is not None:
            s = s + bias
        score[place] = s
        top = jnp.max(s, axis=0, keepdims=True)
        peak = top if peak is None else jnp.maximum(peak, top)
    norm = None
    scale = factor * math.log2(math.e)
    for i, (k_ref, v_ref, rows, _) in enumerate(chunks):
        place = slice(i * half, (i + 1) * half)
        raised = jnp.exp2((score[place] - peak) * scale)
        score[place] = raised
        part = jnp.sum(raised, axis=0, keepdims=True)
        norm = part if norm is None else norm + part
        prob_grad[place] = dot_nt(v_ref[rows], grad)
    inverse = 1.0 / norm
    attended = None
    for i in range(4):
        place = slice(i * half, (i + 1) * half)
        w = (score[place] * inverse).astype(jnp.bfloat16)
        weight[place] = w
        term = dot32(vt[:, place], w)
        attended = term if attended is None else attended + term
        dv_acc[place] += dot32(w, grad)
    attended = attended.T.astype(jnp.bfloat16)
    att_ref[...] = attended
    dots = jnp.sum((grad.astype(jnp.float32) * attended.astype(jnp.float32)).T, axis=0, keepdims=True)
    query_grad = None
    for i in range(4):
        place = slice(i * half, (i + 1) * half)
        ds = (weight[place].astype(jnp.float32) * (prob_grad[place] - dots)).astype(jnp.bfloat16)
        term = dot32(kt[:, place], ds)
        query_grad = term if query_grad is None else query_grad + term
        dk_acc[place] += dot32(ds, query)
    query_grad = query_grad.T * factor
    qpart_ref[...] = norm_back(raw, inverse_rms, gain, query_grad).astype(jnp.bfloat16)

    @pl.when(step == last)
    def _():
        dkp_ref[...] = (dk_acc[0:half] * factor).astype(jnp.bfloat16)
        dvp_ref[...] = dv_acc[0:half].astype(jnp.bfloat16)
        dk_ref[...] = dk_acc[half : 3 * half] * factor
        dv_ref[...] = dv_acc[half : 3 * half]
        dkn_ref[...] = (dk_acc[3 * half : total] * factor).astype(jnp.bfloat16)
        dvn_ref[...] = dv_acc[3 * half : total].astype(jnp.bfloat16)


def attend(bias, gain, raw, grad, kp, ko, kn, vp, vo, vn):
    rows, local = raw.shape
    heads, half = local // HEAD_DIM, rows // 2
    block = min(256, rows)
    by_row = pl.BlockSpec((block, HEAD_DIM), lambda h, j: (j, h))
    own = pl.BlockSpec((rows, HEAD_DIM), lambda h, j: (0, h))
    edge = pl.BlockSpec((half, HEAD_DIM), lambda h, j: (0, h))
    full = jax.ShapeDtypeStruct((rows, local), jnp.bfloat16)
    full32 = jax.ShapeDtypeStruct((rows, local), jnp.float32)
    edge_shape = jax.ShapeDtypeStruct((half, local), jnp.bfloat16)
    window = 2 * rows
    flops = 12 * rows * window * local
    return pl.pallas_call(
        attend_kernel,
        grid=(heads, rows // block),
        in_specs=[
            pl.BlockSpec(memory_space=pltpu.SMEM),
            pl.BlockSpec(gain.shape, lambda h, j: (0, 0)),
            by_row, by_row, edge, own, edge, edge, own, edge,
        ],
        out_specs=(by_row, by_row, own, own, edge, edge, edge, edge),
        out_shape=(full, full, full32, full32, edge_shape, edge_shape, edge_shape, edge_shape),
        scratch_shapes=[
            pltpu.VMEM((HEAD_DIM, window), jnp.bfloat16),
            pltpu.VMEM((HEAD_DIM, window), jnp.bfloat16),
            pltpu.VMEM((window, block), jnp.float32),
            pltpu.VMEM((window, block), jnp.float32),
            pltpu.VMEM((window, block), jnp.bfloat16),
            pltpu.VMEM((window, block), jnp.bfloat16),
            pltpu.VMEM((window, HEAD_DIM), jnp.float32),
            pltpu.VMEM((window, HEAD_DIM), jnp.float32),
        ],
        compiler_params=pltpu.CompilerParams(
            dimension_semantics=("arbitrary", "arbitrary"), vmem_limit_bytes=40 * 1024 * 1024
        ),
        cost_estimate=pl.CostEstimate(
            flops=flops, bytes_accessed=16 * rows * local, transcendentals=rows * window * heads
        ),
        name="attend",
    )(bias, gain, raw, grad, kp, ko, kn, vp, vo, vn)

MESH = pl.DeviceIdType.MESH


def halving_orders(count, streams):
    bits = [1 << i for i in range(count.bit_length() - 1)]
    rest = bits[1:]
    orders = []
    for s in range(streams):
        turn = s % max(1, len(rest))
        orders.append(bits[:1] + rest[turn:] + rest[:turn])
    return orders


def subsets(bits):
    if not bits:
        return [0]
    tail = subsets(bits[1:])
    return [bits[0] | t for t in tail] + tail


def summed_kernel(count, streams, *refs):
    terms, outs = refs[:streams], refs[streams : 2 * streams]
    landed, send_sems, recv_sems = refs[2 * streams :]
    me = lax.axis_index("frame")
    rows = outs[0].shape[0]
    bits = [1 << i for i in range(count.bit_length() - 1)]
    shift = {b: b - 2 * b * (lax.div(me, b) % 2) for b in bits}

    barrier = pltpu.get_barrier_semaphore()
    for b in bits:
        pl.semaphore_signal(barrier, inc=1, device_id={"frame": me + shift[b]}, device_id_type=MESH)
    pl.semaphore_wait(barrier, len(bits))

    def block_of(term, relative):
        place = me
        for b in bits:
            if relative & b:
                place = place + shift[b]
        return term.at[pl.ds(pl.multiple_of(place * rows, rows), rows)]

    orders = halving_orders(count, streams)
    slots = [{} for _ in range(streams)]
    copies = [{} for _ in range(streams)]
    for s in range(streams):
        for k in range(len(bits)):
            for rest in subsets(orders[s][k + 1 :]):
                slots[s][k, rest] = len(slots[s])
    for k in range(len(bits)):
        lists = [subsets(orders[s][k + 1 :]) for s in range(streams)]
        for j in range(len(lists[0])):
            for s in range(streams):
                rest, bit = lists[s][j], orders[s][k]
                relative = rest | bit
                source = block_of(terms[s], relative)
                if k:
                    total = source[...].astype(jnp.float32)
                    for earlier in range(k):
                        copies[s][earlier, relative].wait_recv()
                        total += landed[s, slots[s][earlier, relative]].astype(jnp.float32)
                    slot = slots[s][k - 1, relative]
                    landed[s, slot] = total.astype(landed.dtype)
                    source = landed.at[s, slot]
                slot = slots[s][k, rest]
                copies[s][k, rest] = pltpu.make_async_remote_copy(
                    src_ref=source,
                    dst_ref=landed.at[s, slot],
                    send_sem=send_sems.at[s, slot],
                    recv_sem=recv_sems.at[s, slot],
                    device_id={"frame": me + shift[bit]},
                    device_id_type=MESH,
                )
                copies[s][k, rest].start()
    for s in range(streams):
        total = block_of(terms[s], 0)[...].astype(jnp.float32)
        for k in range(len(bits)):
            copies[s][k, 0].wait_recv()
            total += landed[s, slots[s][k, 0]].astype(jnp.float32)
        outs[s][...] = total
    for s in range(streams):
        for copy in copies[s].values():
            copy.wait_send()


def summed_over_frames(*terms):
    count, streams = lax.axis_size("frame"), len(terms)
    depth, local = terms[0].shape
    rows = depth // count
    vmem = pl.BlockSpec(memory_space=pltpu.VMEM)
    shape = jax.ShapeDtypeStruct((rows, local), jnp.float32)
    return pl.pallas_call(
        functools.partial(summed_kernel, count, streams),
        in_specs=[vmem] * streams,
        out_specs=(vmem,) * streams,
        out_shape=(shape,) * streams,
        scratch_shapes=[
            pltpu.VMEM((streams, count - 1, rows, local), terms[0].dtype),
            pltpu.SemaphoreType.DMA((streams, count - 1)),
            pltpu.SemaphoreType.DMA((streams, count - 1)),
        ],
        compiler_params=pltpu.CompilerParams(
            collective_id=0, has_side_effects=True, vmem_limit_bytes=40 * 1024 * 1024
        ),
        name="summed",
    )(*terms)


def per_device(hidden, qkv_weight, norm_gain, out_grad):
    gathered = lax.all_gather(hidden, "tensor", axis=0, tiled=True)
    rows = gathered.shape[0]
    half = rows // 2
    wq, wk, wv = (qkv_weight[:, i] for i in range(3))
    key_raw = dot32(gathered, wk)
    values = dot32(gathered, wv).astype(jnp.bfloat16)
    keys = key_norm(key_raw, norm_gain)
    kp, vp = (ppermute_by(a[rows - half :], "frame", 1) for a in (keys, values))
    kn, vn = (ppermute_by(a[:half], "frame", -1) for a in (keys, values))
    query_raw = dot32(gathered, wq)
    index, count = (lax.axis_index("frame"), lax.axis_size("frame"))
    bias = jnp.stack(
        [jnp.where(index > 0, 0.0, MASKED), jnp.where(index < count - 1, 0.0, MASKED)]
    ).astype(jnp.float32)
    attended, query_part, dk, dv, dkp, dvp, dkn, dvn = attend(
        bias, norm_gain, query_raw, out_grad, kp, keys, kn, vp, values, vn
    )
    from_next = [ppermute_by(a, "frame", -1) for a in (dkp, dvp)]
    from_prev = [ppermute_by(a, "frame", 1) for a in (dkn, dvn)]

    def weight_term(grads):
        term = lax.dot_general(
            gathered, grads, (((0,), (0,)), ((), ())), preferred_element_type=jnp.float32
        )
        return term.astype(jnp.bfloat16)

    def scattered(term):
        return lax.psum_scatter(term, "frame", scatter_dimension=0, tiled=True)

    query_weight = scattered(weight_term(query_part))
    key_part, value_part = key_back(
        dk, dv, from_prev[0], from_prev[1], from_next[0], from_next[1], key_raw, norm_gain
    )
    key_weight, value_weight = summed_over_frames(weight_term(key_part), weight_term(value_part))
    weight_grad = jnp.stack([query_weight.astype(jnp.float32), key_weight, value_weight], 1)
    return (attended, weight_grad)


def solution(mesh):
    placed = (P(("frame", "tensor"), None), P(None, None, "tensor"), P(), P("frame", "tensor"))
    return jax.shard_map(
        per_device,
        mesh=mesh,
        in_specs=placed,
        out_specs=(P("frame", "tensor"), P("frame", None, "tensor")),
        check_vma=False,
    )
```

time: 562 us -> 402 us (0.72); the launches traced: 555 us -> 401 us
  Pallas kernels: 0 us -> 172 us
  waiting for transfers between devices: 240 us -> 130 us
  matrix products: 157 us -> 52.8 us
  other arithmetic: 62.7 us -> 3.24 us
  local copies, waits for them, and re-layouts: 48.6 us -> 9.5 us
  starting transfers between devices: 33.2 us -> 19 us
    pallas_call x0 -> x4, Pallas kernels: none -> 172 us  [the longest x1 83.8 us: summed_over_frames(): pl.pallas_call(functools.partial(summed_kernel, count, streams), in_specs...]
    unnamed x5 -> x2, waiting for transfers between devices: 118 us -> 0.7 us
    dot_general x13 -> x6, matrix products: 129 us -> 52.8 us  [the longest x3 27.4 us: dot32(): return jnp.dot(left, right, preferred_element_type=jnp.float32)]
    convert_element_type x5 -> x0, other arithmetic: 34.2 us -> none  [the longest x2 28.8 us: window_attention(): (raised / jnp.sum(raised, axis=-1, keepdims=True)).astype(jnp.bfloat16)]
    unnamed x69 -> x38, local copies, waits for them, and re-layouts: 36.4 us -> 6.76 us
    sub x2 -> x0, matrix products: 28.1 us -> none  [window_attention(): raised = jnp.exp(scores - peak)]
    ppermute x4 -> x8, starting transfers between devices: 32.9 us -> 19 us  [ppermute_by(): lax.ppermute(value, axis, [(source, source + steps) for source in range(i...]
    mul x4 -> x0, local copies, waits for them, and re-layouts: 7.02 us -> none  [the longest x2 6.26 us: window_attention(): query_grad = product('hqk,khd->qhd', score_grads, keys) * factor]
  transfers between devices with their start and end apart: 7 -> 10, of which waited for: 5 -> 3; matrix products, arithmetic and copies ran while one was open for 12% -> 8% of each run, Pallas kernels for 0% -> 24%
where the time goes in v1:
time: 402 us; the launch traced here: 401 us
  Pallas kernels  172 us (43%)
  waiting for transfers between devices  130 us (32%)
  matrix products  52.8 us (13%)
  starting transfers between devices  19 us (5%)
  between operations  14.3 us (4%)
  local copies, waits for them, and re-layouts  9.5 us (2%)
    all_gather x1, waiting for transfers between devices, per_device(): gathered = lax.all_gather(hidden, 'tensor', axis=0, tiled=True)  120 us
    pallas_call x1, Pallas kernels, summed_over_frames(): pl.pallas_call(functools.partial(summed_kernel, count, streams), in_specs...  83.8 us
    pallas_call x1, Pallas kernels, attend(): pl.pallas_call(attend_kernel, grid=(heads, rows // block), in_specs=[pl.B...  74.5 us
    dot_general x3, matrix products, dot32(): return jnp.dot(left, right, preferred_element_type=jnp.float32)  27.4 us
    dot_general x3, matrix products, weight_term(): lax.dot_general(gathered, grads, (((0,), (0,)), ((), ())), preferred_elem...  25.4 us
    ppermute x8, starting transfers between devices, ppermute_by(): lax.ppermute(value, axis, [(source, source + steps) for source in range(i...  19 us
    ppermute x8, waiting for transfers between devices, ppermute_by(): lax.ppermute(value, axis, [(source, source + steps) for source in range(i...  9.77 us
    pallas_call x1, Pallas kernels, key_back(): pl.pallas_call(key_back_kernel, grid=(local // HEAD_DIM,), in_specs=[spec...  8.56 us
  transfers between devices with their start and end apart: 10, of which 3 were waited for; matrix products, arithmetic and copies ran while one was open for 8% of the time, Pallas kernels for 24%

profile of v1, /device:TPU:0, one launch (start us, length us, event | category | flops | bytes accessed | tf_op | source)
XLA Modules:
  0.0 401.2 jit_solution(1410192099819807293)
XLA Ops:
  7.2 0.0 all-gather.2.cloned.1.call-start
  7.2 0.7 all-gather.2.cloned.1.call-update
  7.9 0.0 reduce-scatter.2.cloned.1.call-start
  8.0 0.1 pad_maximum_fusion.1.bias_ref
  8.0 119.6 %all-gather.2.cloned.1.call-done = bf16[1024,3072]{1,0:T(8,128)(2,1)} async-done(((bf16[256,3072]{1,0:T(8,128)(2,1)}), bf16[1024,3072]{1,0:T(8,128)(2,1)}) %all-gather.2.cloned.1.call-update) | async-done | bytes 6291472 | tf_op jit(solution)/shard_map/all_gather | solution.py:312
  127.6 8.7 %fusion.12.vo_ref = bf16[1024,768]{1,0:T(8,128)(2,1)S(1)} fusion(bf16[1024,3072]{1,0:T(8,128)(2,1)} %all-gather.2.cloned.1.call-done, bf16[3072,3,768]{2,0,1:T(8,128)(2,1)} %param.5), kind=kOutput, calls=%fused_computation.16 | convolution fusion | flops 4832624640 | bytes 12582912 | tf_op jit(solution)/shard_map/dot_general | solution.py:34
  136.3 1.3 fusion.15
  137.6 1.3 collective-permute-start.3
  138.9 3.1 collective-permute-start.2
  141.9 9.1 %fusion.2.raw_ref = f32[1024,768]{1,0:T(8,128)} fusion(bf16[1024,3072]{1,0:T(8,128)(2,1)S(1)} %copy-done.15, bf16[3072,3,768]{2,0,1:T(8,128)(2,1)} %param.5), kind=kOutput, calls=%fused_computation.5 | convolution fusion | flops 4831838208 | bytes 14155776 | tf_op jit(solution)/shard_map/dot_general | solution.py:34
  151.1 5.4 %key_norm.1.ko_ref = bf16[1024,768]{1,0:T(8,128)(2,1)} custom-call(f32[1024,768]{1,0:T(8,128)} %fusion.2.raw_ref, f32[2,128]{1,0:T(2,128)} %gain_ref.5), custom_call_target="tpu_custom_call" | custom-call | tf_op jit(solution)/shard_map/key_norm/pallas_call | solution.py:49
  156.4 1.5 fusion.16
  157.9 1.3 collective-permute-start.1
  159.2 0.0 copy-start
  159.2 0.0 copy-start.1
  159.2 0.0 copy-start.2
  159.3 4.2 %collective-permute-start = (bf16[512,768]{1,0:T(8,128)(2,1)S(1)}, bf16[512,768]{1,0:T(8,128)(2,1)S(1)}, u32[]{:S(2)}, u32[]{:S(2)}) collective-permute-start(bf16[512,768]{1,0:T(8,128)(2,1)S(1)} %get-tuple-element.29), channel_id=1, source_target_pairs={{0,4},{4,8},{8,12},{12,16},{16,20},{20,24},{24,28},{1,5},{5,9},{9,... | collective-permute-start | bytes 2359304 | tf_op jit(solution)/shard_map/ppermute | solution.py:20
  163.5 9.7 %fusion.4.raw_ref = f32[1024,768]{1,0:T(8,128)} fusion(bf16[1024,3072]{1,0:T(8,128)(2,1)} %all-gather.2.cloned.1.call-done, bf16[3072,3,768]{2,0,1:T(8,128)(2,1)} %param.5), kind=kOutput, calls=%fused_computation.7 | convolution fusion | flops 4831838208 | bytes 14155776 | tf_op jit(solution)/shard_map/dot_general | solution.py:34
  173.1 0.0 collective-permute-done.3.vn_ref
  173.1 0.0 collective-permute-done.2.vp_ref
  173.2 0.9 copy-done.7
  174.0 0.0 collective-permute-done.1.kn_ref
  174.0 0.0 collective-permute-done.kp_ref
  174.1 1.1 copy-done.8
  175.2 74.5 %attend.1 = (bf16[1024,768]{1,0:T(8,128)(2,1)}, bf16[1024,768]{1,0:T(8,128)(2,1)S(1)}, f32[1024,768]{1,0:T(8,128)}, f32[1024,768]{1,0:T(8,128)}, bf16[512,768]{1...) custom-call(f32[2]{0:T(128)S(1)} %pad_maximum_fusion.1.bias_ref, ...), custom_call_target="tpu_custom_call" | custom-call | flops 19327352832 | bytes 12582912 | tf_op jit(solution)/shard_map/attend/pallas_call | solution.py:176
  249.7 0.9 copy-done.3
  250.6 0.9 copy-done.5
  251.5 0.9 copy-done.9
  252.3 12.0 %fusion.9 = bf16[3072,768]{1,0:T(8,128)(2,1)} fusion(bf16[1024,768]{1,0:T(8,128)(2,1)S(1)} %get-tuple-element.15, bf16[1024,3072]{1,0:T(8,128)(2,1)} %all-gather.2.cloned.1.call-done), kind=kOutput, calls=%fused_computation.12 | convolution fusion | flops 4834197504 | bytes 12582912 | tf_op jit(solution)/shard_map/dot_general | solution.py:333
  264.3 0.0 reduce-scatter.2.cloned.1.call-update
  264.3 1.1 copy-done.10
  265.4 3.8 collective-permute-start.4
  269.3 0.0 copy-done.6
  269.3 2.4 collective-permute-start.5
  271.7 1.3 collective-permute-start.6
  273.0 1.5 collective-permute-start.7
  274.6 0.0 collective-permute-done.4.pk_ref
  274.6 0.0 collective-permute-done.5.pv_ref
  274.6 7.8 %collective-permute-done.6.nk_ref = bf16[512,768]{1,0:T(8,128)(2,1)S(1)} collective-permute-done((bf16[512,768]{1,0:T(8,128)(2,1)S(1)}, bf16[512,768]{1,0:T(8,128)(2,1)S(1)}, u32[]{:S(2)}, u32[]{:S(2)}) %collective-permute-start.6) | collective-permute-done | bytes 786464 | tf_op jit(solution)/shard_map/ppermute | solution.py:20
  282.4 1.9 collective-permute-done.7.nv_ref
  284.4 0.9 copy-done.14
  285.3 8.6 %key_back.1 = (bf16[1024,768]{1,0:T(8,128)(2,1)}, bf16[1024,768]{1,0:T(8,128)(2,1)}) custom-call(f32[1024,768]{1,0:T(8,128)} %get-tuple-element.16.dk_ref, f32[1024,768]{1,0:T(8,128)} %get-tuple-element.17.dv_ref, bf16[512,768]{1,0:T(8,128)(2,1)} %copy-done.11, bf16[512,768]{1,0:T(8,128)(2,1)} %copy-done.12, bf16[512,768]{1,0:T(8,128)(2,1)} %copy-done.13, ...), custom_call_target="tpu_custom_call" | custom-call | tf_op jit(solution)/shard_map/key_back/pallas_call | solution.py:75
  293.9 7.9 %fusion.10.refs_0_ = bf16[3072,768]{1,0:T(8,128)(2,1)S(1)} fusion(bf16[1024,768]{1,0:T(8,128)(2,1)} %get-tuple-element.22, bf16[1024,3072]{1,0:T(8,128)(2,1)} %all-gather.2.cloned.1.call-done), kind=kOutput, calls=%fused_computation.13 | convolution fusion | flops 4834197504 | bytes 12582912 | tf_op jit(solution)/shard_map/dot_general | solution.py:333
  301.8 5.6 %fusion.11.refs_1_ = bf16[3072,768]{1,0:T(8,128)(2,1)S(1)} fusion(bf16[1024,768]{1,0:T(8,128)(2,1)S(1)} %copy-done.16, bf16[1024,3072]{1,0:T(8,128)(2,1)S(1)} %bitcast.36), kind=kOutput, calls=%fused_computation.14 | convolution fusion | flops 4834197504 | bytes 12582912 | tf_op jit(solution)/shard_map/dot_general | solution.py:333
  307.4 83.8 %summed.1 = (f32[384,768]{1,0:T(8,128)S(1)}, f32[384,768]{1,0:T(8,128)S(1)}) custom-call(bf16[3072,768]{1,0:T(8,128)(2,1)S(1)} %fusion.10.refs_0_, bf16[3072,768]{1,0:T(8,128)(2,1)S(1)} %fusion.11.refs_1_), custom_call_target="tpu_custom_call" | custom-call | tf_op jit(solution)/shard_map/summed/pallas_call | solution.py:294
  391.1 0.0 reduce-scatter.2.cloned.1.call-done
  391.2 1.1 bitcast_convert_fusion
  392.3 2.0 pad_maximum_fusion
  (28 shorter events, 0.1 us)
Async XLA Ops:
  7.2 120.5 %all-gather.2.cloned.1.call-start = ((), (), s32[]{:S(2)}) async-start(), calls=%async_computation.1 | async-start | bytes 7864320 | tf_op jit(solution)/shard_map/all_gather | solution.py:312
  7.9 383.3 %reduce-scatter.2.cloned.1.call-start = ((), (), s32[]{:S(2)}) async-start(), calls=%async_computation.2 | async-start | bytes 5308416 | tf_op jit(solution)/shard_map/reduce_scatter | solution.py:339
  127.6 14.3 %copy-start.15 = (bf16[1024,3072]{1,0:T(8,128)(2,1)S(1)}, bf16[1024,3072]{1,0:T(8,128)(2,1)}, u32[]{:S(2)}) copy-start(bf16[1024,3072]{1,0:T(8,128)(2,1)} %all-gather.2.cloned.1.call-done) | copy-start | bytes 18874372
  137.6 35.6 %collective-permute-start.3 = (bf16[512,768]{1,0:T(8,128)(2,1)}, bf16[512,768]{1,0:T(8,128)(2,1)S(1)}, u32[]{:S(2)}, u32[]{:S(2)}) collective-permute-start(bf16[512,768]{1,0:T(8,128)(2,1)} %get-tuple-element.26), channel_id=1, source_target_pairs={{4,0},{8,4},{12,8},{16,12},{20,16},{24,20},{28,24},{5,1},{9,5},{13... | collective-permute-start | bytes 2359304 | tf_op jit(solution)/shard_map/ppermute | solution.py:20
  138.9 34.3 %collective-permute-start.2 = (bf16[512,768]{1,0:T(8,128)(2,1)}, bf16[512,768]{1,0:T(8,128)(2,1)S(1)}, u32[]{:S(2)}, u32[]{:S(2)}) collective-permute-start(bf16[512,768]{1,0:T(8,128)(2,1)} %get-tuple-element.27), channel_id=1, source_target_pairs={{0,4},{4,8},{8,12},{12,16},{16,20},{20,24},{24,28},{1,5},{5,9},{9,... | collective-permute-start | bytes 2359304 | tf_op jit(solution)/shard_map/ppermute | solution.py:20
  157.9 16.1 %collective-permute-start.1 = (bf16[512,768]{1,0:T(8,128)(2,1)S(1)}, bf16[512,768]{1,0:T(8,128)(2,1)S(1)}, u32[]{:S(2)}, u32[]{:S(2)}) collective-permute-start(bf16[512,768]{1,0:T(8,128)(2,1)S(1)} %get-tuple-element.28), channel_id=1, source_target_pairs={{4,0},{8,4},{12,8},{16,12},{20,16},{24,20},{28,24},{5,1},{9,5},{13... | collective-permute-start | bytes 2359304 | tf_op jit(solution)/shard_map/ppermute | solution.py:20
  159.2 14.8 %copy-start = (bf16[1024,768]{1,0:T(8,128)(2,1)S(1)}, bf16[1024,768]{1,0:T(8,128)(2,1)}, u32[]{:S(2)}) copy-start(bf16[1024,768]{1,0:T(8,128)(2,1)} %key_norm.1.ko_ref) | copy-start | bytes 4718596
  159.2 14.8 %copy-start.1 = (f32[2,128]{1,0:T(2,128)S(1)}, f32[2,128]{1,0:T(2,128)}, u32[]{:S(2)}) copy-start(f32[2,128]{1,0:T(2,128)} %gain_ref.5) | copy-start | bytes 3076
  159.2 14.8 %copy-start.2 = (bf16[1024,768]{1,0:T(8,128)(2,1)S(1)}, bf16[1024,768]{1,0:T(8,128)(2,1)}, u32[]{:S(2)}) copy-start(bf16[1024,768]{1,0:T(8,128)(2,1)} %grad_ref.1) | copy-start | bytes 4718596
  159.3 14.8 %collective-permute-start = (bf16[512,768]{1,0:T(8,128)(2,1)S(1)}, bf16[512,768]{1,0:T(8,128)(2,1)S(1)}, u32[]{:S(2)}, u32[]{:S(2)}) collective-permute-start(bf16[512,768]{1,0:T(8,128)(2,1)S(1)} %get-tuple-element.29), channel_id=1, source_target_pairs={{0,4},{4,8},{8,12},{12,16},{16,20},{20,24},{24,28},{1,5},{5,9},{9,... | collective-permute-start | bytes 2359304 | tf_op jit(solution)/shard_map/ppermute | solution.py:20
  173.2 0.9 copy-start.7
  174.1 1.1 copy-start.8
  249.7 0.9 copy-start.3
  250.6 0.9 copy-start.5
  251.5 0.9 copy-start.9
  264.3 1.1 copy-start.10
  264.3 5.0 %copy-start.6 = (bf16[512,768]{1,0:T(8,128)(2,1)S(1)}, bf16[512,768]{1,0:T(8,128)(2,1)}, u32[]{:S(2)}) copy-start(bf16[512,768]{1,0:T(8,128)(2,1)} %copy-done.5) | copy-start | bytes 2359300
  264.3 7.4 %copy-start.4 = (bf16[512,768]{1,0:T(8,128)(2,1)S(1)}, bf16[512,768]{1,0:T(8,128)(2,1)}, u32[]{:S(2)}) copy-start(bf16[512,768]{1,0:T(8,128)(2,1)} %copy-done.3) | copy-start | bytes 2359300
  265.4 9.1 %collective-permute-start.4 = (bf16[512,768]{1,0:T(8,128)(2,1)S(1)}, bf16[512,768]{1,0:T(8,128)(2,1)S(1)}, u32[]{:S(2)}, u32[]{:S(2)}) collective-permute-start(bf16[512,768]{1,0:T(8,128)(2,1)S(1)} %copy-done.10), channel_id=1, source_target_pairs={{0,4},{4,8},{8,12},{12,16},{16,20},{20,24},{24,28},{1,5},{5,9},{9,... | collective-permute-start | bytes 2359304 | tf_op jit(solution)/shard_map/ppermute | solution.py:20
  269.3 5.3 %collective-permute-start.5 = (bf16[512,768]{1,0:T(8,128)(2,1)S(1)}, bf16[512,768]{1,0:T(8,128)(2,1)S(1)}, u32[]{:S(2)}, u32[]{:S(2)}) collective-permute-start(bf16[512,768]{1,0:T(8,128)(2,1)S(1)} %copy-done.6), channel_id=1, source_target_pairs={{0,4},{4,8},{8,12},{12,16},{16,20},{20,24},{24,28},{1,5},{5,9},{9,... | collective-permute-start | bytes 2359304 | tf_op jit(solution)/shard_map/ppermute | solution.py:20
  271.7 10.7 %collective-permute-start.6 = (bf16[512,768]{1,0:T(8,128)(2,1)S(1)}, bf16[512,768]{1,0:T(8,128)(2,1)S(1)}, u32[]{:S(2)}, u32[]{:S(2)}) collective-permute-start(bf16[512,768]{1,0:T(8,128)(2,1)S(1)} %copy-done.4), channel_id=1, source_target_pairs={{4,0},{8,4},{12,8},{16,12},{20,16},{24,20},{28,24},{5,1},{9,5},{13... | collective-permute-start | bytes 2359304 | tf_op jit(solution)/shard_map/ppermute | solution.py:20
  273.0 11.3 %collective-permute-start.7 = (bf16[512,768]{1,0:T(8,128)(2,1)S(1)}, bf16[512,768]{1,0:T(8,128)(2,1)S(1)}, u32[]{:S(2)}, u32[]{:S(2)}) collective-permute-start(bf16[512,768]{1,0:T(8,128)(2,1)S(1)} %get-tuple-element.21), channel_id=1, source_target_pairs={{4,0},{8,4},{12,8},{16,12},{20,16},{24,20},{28,24},{5,1},{9,5},{13... | collective-permute-start | bytes 2359304 | tf_op jit(solution)/shard_map/ppermute | solution.py:20
  274.6 9.8 %copy-start.11 = (bf16[512,768]{1,0:T(8,128)(2,1)}, bf16[512,768]{1,0:T(8,128)(2,1)S(1)}, u32[]{:S(2)}) copy-start(bf16[512,768]{1,0:T(8,128)(2,1)S(1)} %collective-permute-done.4.pk_ref) | copy-start | bytes 2359300
  274.6 9.8 %copy-start.12 = (bf16[512,768]{1,0:T(8,128)(2,1)}, bf16[512,768]{1,0:T(8,128)(2,1)S(1)}, u32[]{:S(2)}) copy-start(bf16[512,768]{1,0:T(8,128)(2,1)S(1)} %collective-permute-done.5.pv_ref) | copy-start | bytes 2359300
  282.4 1.9 copy-start.13
  284.4 1.0 copy-start.14
  285.3 16.5 %slice-start = ((s8[6291456]{0:T(1024)(128)(4,1)}), s8[2097152]{0:T(1024)(128)(4,1)S(1)}, s32[]{:S(2)}) async-start(s8[6291456]{0:T(1024)(128)(4,1)} %bitcast.35), calls=%async_computation.3 | async-start | bytes 4194304
  293.9 7.9 %slice-start.1 = ((s8[6291456]{0:T(1024)(128)(4,1)}), s8[4194304]{0:T(1024)(128)(4,1)S(1)}, s32[]{:S(2)}) async-start(s8[6291456]{0:T(1024)(128)(4,1)} %bitcast.35), calls=%async_computation.4 | async-start | bytes 8388608
  293.9 7.9 %copy-start.16 = (bf16[1024,768]{1,0:T(8,128)(2,1)S(1)}, bf16[1024,768]{1,0:T(8,128)(2,1)}, u32[]{:S(2)}) copy-start(bf16[1024,768]{1,0:T(8,128)(2,1)} %get-tuple-element.23) | copy-start | bytes 4718596
Sparse Core Ops, SparseCore 0:
  9.5 118.0 all-gather.1
  264.5 71.2 reduce-scatter.1

commit v2 on v1

--- a/solution.py
+++ b/solution.py
@@ -36,24 +36,6 @@
 
 def dot_nt(left, right):
     return lax.dot_general(left, right, NT, preferred_element_type=jnp.float32)
-
-
-def key_norm_kernel(raw_ref, gain_ref, out_ref):
-    raw = raw_ref[...]
-    out_ref[...] = (raw * inverse_rms_of(raw) * gain_ref[1:2]).astype(out_ref.dtype)
-
-
-def key_norm(raw, gain):
-    rows, local = raw.shape
-    spec = pl.BlockSpec((rows, HEAD_DIM), lambda h: (0, h))
-    return pl.pallas_call(
-        key_norm_kernel,
-        grid=(local // HEAD_DIM,),
-        in_specs=[spec, pl.BlockSpec(gain.shape, lambda h: (0, 0))],
-        out_specs=spec,
-        out_shape=jax.ShapeDtypeStruct(raw.shape, jnp.bfloat16),
-        name="key_norm",
-    )(raw, gain)
 
 
 def key_back_kernel(dk_ref, dv_ref, pk_ref, pv_ref, nk_ref, nv_ref, raw_ref, gain_ref, kout_ref, vout_ref):
@@ -222,11 +204,12 @@
     return [bits[0] | t for t in tail] + tail
 
 
-def summed_kernel(count, streams, *refs):
-    terms, outs = refs[:streams], refs[streams : 2 * streams]
-    landed, send_sems, recv_sems = refs[2 * streams :]
+def summed_kernel(count, number, *refs):
+    terms, outs = refs[:number], refs[number : 2 * number]
+    landed, send_sems, recv_sems = refs[2 * number :]
     me = lax.axis_index("frame")
-    rows = outs[0].shape[0]
+    full = outs[0].shape[0]
+    streams, rows = 2 * number, full // 2
     bits = [1 << i for i in range(count.bit_length() - 1)]
     shift = {b: b - 2 * b * (lax.div(me, b) % 2) for b in bits}
 
@@ -235,12 +218,13 @@
         pl.semaphore_signal(barrier, inc=1, device_id={"frame": me + shift[b]}, device_id_type=MESH)
     pl.semaphore_wait(barrier, len(bits))
 
-    def block_of(term, relative):
+    def block_of(stream, relative):
         place = me
         for b in bits:
             if relative & b:
                 place = place + shift[b]
-        return term.at[pl.ds(pl.multiple_of(place * rows, rows), rows)]
+        first = pl.multiple_of(place * full + (stream % 2) * rows, rows)
+        return terms[stream // 2].at[pl.ds(first, rows)]
 
     orders = halving_orders(count, streams)
     slots = [{} for _ in range(streams)]
@@ -255,7 +239,7 @@
             for s in range(streams):
                 rest, bit = lists[s][j], orders[s][k]
                 relative = rest | bit
-                source = block_of(terms[s], relative)
+                source = block_of(s, relative)
                 if k:
                     total = source[...].astype(jnp.float32)
                     for earlier in range(k):
@@ -275,31 +259,31 @@
                 )
                 copies[s][k, rest].start()
     for s in range(streams):
-        total = block_of(terms[s], 0)[...].astype(jnp.float32)
+        total = block_of(s, 0)[...].astype(jnp.float32)
         for k in range(len(bits)):
             copies[s][k, 0].wait_recv()
             total += landed[s, slots[s][k, 0]].astype(jnp.float32)
-        outs[s][...] = total
+        outs[s // 2][(s % 2) * rows : (s % 2 + 1) * rows] = total
     for s in range(streams):
         for copy in copies[s].values():
             copy.wait_send()
 
 
 def summed_over_frames(*terms):
-    count, streams = lax.axis_size("frame"), len(terms)
+    count, number = lax.axis_size("frame"), len(terms)
     depth, local = terms[0].shape
     rows = depth // count
     vmem = pl.BlockSpec(memory_space=pltpu.VMEM)
     shape = jax.ShapeDtypeStruct((rows, local), jnp.float32)
     return pl.pallas_call(
-        functools.partial(summed_kernel, count, streams),
-        in_specs=[vmem] * streams,
-        out_specs=(vmem,) * streams,
-        out_shape=(shape,) * streams,
+        functools.partial(summed_kernel, count, number),
+        in_specs=[vmem] * number,
+        out_specs=(vmem,) * number,
+        out_shape=(shape,) * number,
         scratch_shapes=[
-            pltpu.VMEM((streams, count - 1, rows, local), terms[0].dtype),
-            pltpu.SemaphoreType.DMA((streams, count - 1)),
-            pltpu.SemaphoreType.DMA((streams, count - 1)),
+            pltpu.VMEM((2 * number, count - 1, rows // 2, local), terms[0].dtype),
+            pltpu.SemaphoreType.DMA((2 * number, count - 1)),
+            pltpu.SemaphoreType.DMA((2 * number, count - 1)),
         ],
         compiler_params=pltpu.CompilerParams(
             collective_id=0, has_side_effects=True, vmem_limit_bytes=40 * 1024 * 1024
@@ -308,17 +292,124 @@
     )(*terms)
 
 
+def project_kernel(
+    count, gain_ref, hidden_ref, weight_hbm, gathered, query_raw, key_raw, keys, values,
+    weight, weight_sems, send_sems, recv_sems,
+):
+    me = lax.axis_index("tensor")
+    rows = hidden_ref.shape[0]
+    has_left, has_right = me > 0, me < count - 1
+    loads = [
+        pltpu.make_async_copy(weight_hbm.at[i], weight.at[i], weight_sems.at[i]) for i in range(3)
+    ]
+    for load in loads:
+        load.start()
+    barrier = pltpu.get_barrier_semaphore()
+    for there in (lax.rem(me + count - 1, count), lax.rem(me + 1, count)):
+        pl.semaphore_signal(barrier, inc=1, device_id={"tensor": there}, device_id_type=MESH)
+    pl.semaphore_wait(barrier, 2)
+
+    def rows_of(shard):
+        return pl.ds(pl.multiple_of(shard * rows, rows), rows)
+
+    def copy_of(side, step, shard, source):
+        return pltpu.make_async_remote_copy(
+            src_ref=source,
+            dst_ref=gathered.at[rows_of(shard)],
+            send_sem=send_sems.at[side, step],
+            recv_sem=recv_sems.at[side, step],
+            device_id={"tensor": me + 1 - 2 * side},
+            device_id_type=MESH,
+        )
+
+    for side, near in ((0, has_right), (1, has_left)):
+        @pl.when(near)
+        def _(side=side):
+            copy_of(side, 0, me, hidden_ref).start()
+    gathered[rows_of(me)] = hidden_ref[...]
+    for load in loads:
+        load.wait()
+
+    def one_step(step, carry):
+        @pl.when(step > 0)
+        def _():
+            for side, near in ((0, has_right), (1, has_left)):
+                shard = me - step if side == 0 else me + step
+                there = shard >= 0 if side == 0 else shard < count
+
+                @pl.when(there)
+                def _(side=side, shard=shard):
+                    copy_of(side, step - 1, shard, gathered.at[rows_of(shard)]).wait_recv()
+
+                @pl.when(there & near)
+                def _(side=side, shard=shard):
+                    copy_of(side, step, shard, gathered.at[rows_of(shard)]).start()
+
+        def one_side(side, inner):
+            shard = me - step + 2 * step * side
+
+            @pl.when((shard >= 0) & (shard < count) & (step >= side))
+            def _():
+                place = rows_of(shard)
+                tokens = gathered[place]
+                raw = dot32(tokens, weight[1])
+                key_raw[place] = raw
+                for h in range(raw.shape[1] // HEAD_DIM):
+                    columns = slice(h * HEAD_DIM, (h + 1) * HEAD_DIM)
+                    head = raw[:, columns]
+                    normed = head * inverse_rms_of(head) * gain_ref[1:2]
+                    keys[place, columns] = normed.astype(keys.dtype)
+                values[place] = dot32(tokens, weight[2]).astype(values.dtype)
+                query_raw[place] = dot32(tokens, weight[0])
+
+            return inner
+
+        return lax.fori_loop(0, 2, one_side, carry)
+
+    lax.fori_loop(0, count, one_step, 0)
+    for step in range(count - 1):
+        for side, near in ((0, has_right), (1, has_left)):
+            shard = me - step if side == 0 else me + step
+            there = shard >= 0 if side == 0 else shard < count
+
+            @pl.when(there & near)
+            def _(side=side, shard=shard, step=step):
+                source = hidden_ref if step == 0 else gathered.at[rows_of(shard)]
+                copy_of(side, step, shard, source).wait_send()
+
+
+def project(hidden, qkv_weight, gain):
+    count = lax.axis_size("tensor")
+    rows, depth = hidden.shape
+    local = qkv_weight.shape[2]
+    total = rows * count
+    vmem = pl.BlockSpec(memory_space=pltpu.VMEM)
+    wide = jax.ShapeDtypeStruct((total, local), jnp.float32)
+    narrow = jax.ShapeDtypeStruct((total, local), jnp.bfloat16)
+    return pl.pallas_call(
+        functools.partial(project_kernel, count),
+        in_specs=[vmem, vmem, pl.BlockSpec(memory_space=pl.ANY)],
+        out_specs=(vmem,) * 5,
+        out_shape=(jax.ShapeDtypeStruct((total, depth), hidden.dtype), wide, wide, narrow, narrow),
+        scratch_shapes=[
+            pltpu.VMEM((3, depth, local), qkv_weight.dtype),
+            pltpu.SemaphoreType.DMA((3,)),
+            pltpu.SemaphoreType.DMA((2, count)),
+            pltpu.SemaphoreType.DMA((2, count)),
+        ],
+        compiler_params=pltpu.CompilerParams(
+            collective_id=1, has_side_effects=True, vmem_limit_bytes=50 * 1024 * 1024
+        ),
+        name="project",
+    )(gain, hidden, jnp.transpose(qkv_weight, (1, 0, 2)))
+
+
 def per_device(hidden, qkv_weight, norm_gain, out_grad):
-    gathered = lax.all_gather(hidden, "tensor", axis=0, tiled=True)
+    gathered, query_raw, key_raw, keys, values = project(hidden, qkv_weight, norm_gain)
     rows = gathered.shape[0]
     half = rows // 2
-    wq, wk, wv = (qkv_weight[:, i] for i in range(3))
-    key_raw = dot32(gathered, wk)
-    values = dot32(gathered, wv).astype(jnp.bfloat16)
-    keys = key_norm(key_raw, norm_gain)
     kp, vp = (ppermute_by(a[rows - half :], "frame", 1) for a in (keys, values))
     kn, vn = (ppermute_by(a[:half], "frame", -1) for a in (keys, values))
-    query_raw = dot32(gathered, wq)
     index, count = (lax.axis_index("frame"), lax.axis_size("frame"))
     bias = jnp.stack(
         [jnp.where(index > 0, 0.0, MASKED), jnp.where(index < count - 1, 0.0, MASKED)]
@@ -335,15 +426,11 @@
         )
         return term.astype(jnp.bfloat16)
 
-    def scattered(term):
-        return lax.psum_scatter(term, "frame", scatter_dimension=0, tiled=True)
-
-    query_weight = scattered(weight_term(query_part))
     key_part, value_part = key_back(
         dk, dv, from_prev[0], from_prev[1], from_next[0], from_next[1], key_raw, norm_gain
     )
-    key_weight, value_weight = summed_over_frames(weight_term(key_part), weight_term(value_part))
-    weight_grad = jnp.stack([query_weight.astype(jnp.float32), key_weight, value_weight], 1)
+    sums = summed_over_frames(*(weight_term(part) for part in (query_part, key_part, value_part)))
+    weight_grad = jnp.stack(sums, 1)
     return (attended, weight_grad)
 
 

time: 402 us -> 368 us (0.915)
  waiting for transfers between devices: 130 us -> 1.25 us
  Pallas kernels: 172 us -> 292 us
  matrix products: 52.8 us -> 24.6 us
  starting transfers between devices: 19 us -> 39.9 us
  between operations: 14.3 us -> 0.81 us
    pallas_call x2, Pallas kernels: 89.1 us -> 210 us  [the longest x1 118 us: project(): pl.pallas_call(functools.partial(project_kernel, count), in_specs=[vmem,...]
    all_gather x1 -> x0, waiting for transfers between devices: 120 us -> none  [per_device(): gathered = lax.all_gather(hidden, 'tensor', axis=0, tiled=True)]
    dot_general x3 -> x0, matrix products: 27.4 us -> none  [dot32(): return jnp.dot(left, right, preferred_element_type=jnp.float32)]
    ppermute x8, starting transfers between devices: 19 us -> 39.9 us  [ppermute_by(): lax.ppermute(value, axis, [(source, source + steps) for source in range(i...]
    ppermute x8, waiting for transfers between devices: 9.77 us -> 1.25 us  [ppermute_by(): lax.ppermute(value, axis, [(source, source + steps) for source in range(i...]
  transfers between devices with their start and end apart: 10 -> 8, of which waited for: 3 -> 1; matrix products, arithmetic and copies ran while one was open for 8% -> 2% of each run, Pallas kernels for 24% -> 0%
where the time goes in v2:
time: 368 us; the launch traced here: 367 us
  Pallas kernels  292 us (79%)
  starting transfers between devices  39.9 us (11%)
  matrix products  24.6 us (7%)
  local copies, waits for them, and re-layouts  6.24 us (2%)
    pallas_call x1, Pallas kernels, project(): pl.pallas_call(functools.partial(project_kernel, count), in_specs=[vmem,...  118 us
    pallas_call x1, Pallas kernels, summed_over_frames(): pl.pallas_call(functools.partial(summed_kernel, count, number), in_specs=...  91.1 us
    pallas_call x1, Pallas kernels, attend(): pl.pallas_call(attend_kernel, grid=(heads, rows // block), in_specs=[pl.B...  74.5 us
    ppermute x8, starting transfers between devices, ppermute_by(): lax.ppermute(value, axis, [(source, source + steps) for source in range(i...  39.9 us
    dot_general x3, matrix products, weight_term(): lax.dot_general(gathered, grads, (((0,), (0,)), ((), ())), preferred_elem...  24.6 us
    pallas_call x1, Pallas kernels, key_back(): pl.pallas_call(key_back_kernel, grid=(local // HEAD_DIM,), in_specs=[spec...  8.38 us
  transfers between devices with their start and end apart: 8, of which 1 were waited for; matrix products, arithmetic and copies ran while one was open for 2% of the time, Pallas kernels for 0%

profile of v2, /device:TPU:0, one launch (start us, length us, event | category | flops | bytes accessed | tf_op | source)
XLA Modules:
  0.0 367.4 jit_solution(7539058727462310298)
XLA Ops:
  0.6 0.0 copy-start
  0.6 0.7 copy-done
  1.3 118.4 %project.1 = (bf16[1024,3072]{1,0:T(8,128)(2,1)}, f32[1024,768]{1,0:T(8,128)}, f32[1024,768]{1,0:T(8,128)}, bf16[1024,768]{1,0:T(8,128)(2,1)S(1)}, bf16[1024,768]{1,0:T(8,128)(2,1)S(1)}) custom-call(f32[2,128]{1,0:T(2,128)S(1)} %copy-done, bf16[256,3072]{1,0:T(8,128)(2,1)} %hidden_ref.1, bf16[3,3072,768]{2,1,0:T(8,128)(2,1)} %bitcast.17), custom_call_target="tpu_custom_call" | custom-call | tf_op jit(solution)/shard_map/project/pallas_call | solution.py:389
  119.8 0.0 copy-start.1
  119.8 1.2 fusion.1
  121.0 1.3 collective-permute-start.1
  122.3 3.9 %collective-permute-start = (bf16[512,768]{1,0:T(8,128)(2,1)}, bf16[512,768]{1,0:T(8,128)(2,1)}, u32[]{:S(2)}, u32[]{:S(2)}) collective-permute-start(bf16[512,768]{1,0:T(8,128)(2,1)} %get-tuple-element.41), channel_id=1, source_target_pairs={{0,4},{4,8},{8,12},{12,16},{16,20},{20,24},{24,28},{1,5},{5,9},{9,... | collective-permute-start | bytes 2359304 | tf_op jit(solution)/shard_map/ppermute | solution.py:20
  126.2 1.3 fusion
  127.5 1.3 collective-permute-start.3
  128.8 4.0 %collective-permute-start.2 = (bf16[512,768]{1,0:T(8,128)(2,1)}, bf16[512,768]{1,0:T(8,128)(2,1)}, u32[]{:S(2)}, u32[]{:S(2)}) collective-permute-start(bf16[512,768]{1,0:T(8,128)(2,1)} %get-tuple-element.39), channel_id=1, source_target_pairs={{0,4},{4,8},{8,12},{12,16},{16,20},{20,24},{24,28},{1,5},{5,9},{9,... | collective-permute-start | bytes 2359304 | tf_op jit(solution)/shard_map/ppermute | solution.py:20
  132.8 0.1 pad_maximum_fusion.1.bias_ref
  132.8 0.0 collective-permute-done.1.kn_ref
  132.8 0.0 collective-permute-done.kp_ref
  132.8 0.0 collective-permute-done.3.vn_ref
  132.8 1.2 collective-permute-done.2.vp_ref
  134.1 0.0 copy-done.1
  134.1 0.0 copy-start.2
  134.1 1.4 copy-done.2
  135.5 0.0 copy-start.7
  135.5 74.5 %attend.1 = (bf16[1024,768]{1,0:T(8,128)(2,1)}, bf16[1024,768]{1,0:T(8,128)(2,1)S(1)}, f32[1024,768]{1,0:T(8,128)}, f32[1024,768]{1,0:T(8,128)}, bf16[512,768]{1...) custom-call(f32[2]{0:T(128)S(1)} %pad_maximum_fusion.1.bias_ref, ...), custom_call_target="tpu_custom_call" | custom-call | flops 19327352832 | bytes 12582912 | tf_op jit(solution)/shard_map/attend/pallas_call | solution.py:158
  210.0 24.8 %collective-permute-start.4 = (bf16[512,768]{1,0:T(8,128)(2,1)S(1)}, bf16[512,768]{1,0:T(8,128)(2,1)S(1)}, u32[]{:S(2)}, u32[]{:S(2)}) collective-permute-start(bf16[512,768]{1,0:T(8,128)(2,1)S(1)} %get-tuple-element.28), channel_id=1, source_target_pairs={{0,4},{4,8},{8,12},{12,16},{16,20},{20,24},{24,28},{1,5},{5,9},{9,... | collective-permute-start | bytes 2359304 | tf_op jit(solution)/shard_map/ppermute | solution.py:20
  234.8 1.9 collective-permute-start.5
  236.7 1.3 collective-permute-start.6
  238.0 1.5 collective-permute-start.7
  239.5 0.0 copy-done.7
  239.5 6.9 %convolution_convert_fusion.2.refs_0_ = bf16[3072,768]{1,0:T(8,128)(2,1)} fusion(bf16[1024,3072]{1,0:T(8,128)(2,1)S(1)} %copy-done.7, bf16[1024,768]{1,0:T(8,128)(2,1)S(1)} %get-tuple-element.25), kind=kOutput, calls=%fused_computation.2 | convolution fusion | flops 4834197504 | bytes 12582912 | tf_op jit(solution)/shard_map/dot_general | solution.py:424
  246.4 0.0 collective-permute-done.4.pk_ref
  246.4 0.0 copy-start.3
  246.4 0.0 collective-permute-done.5.pv_ref
  246.4 0.0 copy-start.4
  246.5 0.0 collective-permute-done.6.nk_ref
  246.5 0.0 copy-start.5
  246.5 0.0 collective-permute-done.7.nv_ref
  246.5 0.0 copy-start.6
  246.5 0.8 copy-done.3
  247.3 0.3 copy-done.4
  247.6 0.2 copy-done.5
  247.8 0.3 copy-done.6
  248.1 8.4 %key_back.1 = (bf16[1024,768]{1,0:T(8,128)(2,1)}, bf16[1024,768]{1,0:T(8,128)(2,1)}) custom-call(f32[1024,768]{1,0:T(8,128)} %get-tuple-element.26.dk_ref, f32[1024,768]{1,0:T(8,128)} %get-tuple-element.27.dv_ref, bf16[512,768]{1,0:T(8,128)(2,1)} %copy-done.3, bf16[512,768]{1,0:T(8,128)(2,1)} %copy-done.4, bf16[512,768]{1,0:T(8,128)(2,1)} %copy-done.5, ...), custom_call_target="tpu_custom_call" | custom-call | tf_op jit(solution)/shard_map/key_back/pallas_call | solution.py:57
  256.5 0.0 slice-start
  256.5 7.9 %convolution_convert_fusion.1.refs_1_ = bf16[3072,768]{1,0:T(8,128)(2,1)S(1)} fusion(bf16[1024,3072]{1,0:T(8,128)(2,1)} %get-tuple-element.24, bf16[1024,768]{1,0:T(8,128)(2,1)} %get-tuple-element.33), kind=kOutput, calls=%fused_computation.1 | convolution fusion | flops 4834197504 | bytes 12582912 | tf_op jit(solution)/shard_map/dot_general | solution.py:424
  264.4 0.0 slice-start.1
  264.4 0.0 copy-done.8
  264.4 9.8 %convolution_convert_fusion.refs_2_ = bf16[3072,768]{1,0:T(8,128)(2,1)} fusion(bf16[1024,3072]{1,0:T(8,128)(2,1)} %get-tuple-element.24, bf16[1024,768]{1,0:T(8,128)(2,1)S(1)} %copy-done.8), kind=kOutput, calls=%fused_computation | convolution fusion | flops 4834197504 | bytes 12582912 | tf_op jit(solution)/shard_map/dot_general | solution.py:424
  274.2 0.0 slice-done
  274.2 0.0 slice-done.1
  274.2 91.1 %summed.1 = (f32[384,768]{1,0:T(8,128)S(1)}, f32[384,768]{1,0:T(8,128)S(1)}, f32[384,768]{1,0:T(8,128)S(1)}) custom-call(bf16[3072,768]{1,0:T(8,128)(2,1)S(1)} %bitcast.13, bf16[3072,768]{1,0:T(8,128)(2,1)S(1)} %convolution_convert_fusion.1.refs_1_, bf16[3072,768]{1,0:T(8,128)(2,1)} %convolution_convert_fusion.refs_2_), custom_call_target="tpu_custom_call" | custom-call | tf_op jit(solution)/shard_map/summed/pallas_call | solution.py:278
  365.3 2.0 pad_maximum_fusion
  (2 shorter events, 0.0 us)
Async XLA Ops:
  0.6 0.7 copy-start
  119.8 14.3 %copy-start.1 = (f32[2,128]{1,0:T(2,128)S(1)}, f32[2,128]{1,0:T(2,128)}, u32[]{:S(2)}) copy-start(f32[2,128]{1,0:T(2,128)} %gain_ref.5) | copy-start | bytes 3076
  121.0 11.8 %collective-permute-start.1 = (bf16[512,768]{1,0:T(8,128)(2,1)}, bf16[512,768]{1,0:T(8,128)(2,1)}, u32[]{:S(2)}, u32[]{:S(2)}) collective-permute-start(bf16[512,768]{1,0:T(8,128)(2,1)} %get-tuple-element.40), channel_id=1, source_target_pairs={{4,0},{8,4},{12,8},{16,12},{20,16},{24,20},{28,24},{5,1},{9,5},{13... | collective-permute-start | bytes 2359304 | tf_op jit(solution)/shard_map/ppermute | solution.py:20
  122.3 10.5 %collective-permute-start = (bf16[512,768]{1,0:T(8,128)(2,1)}, bf16[512,768]{1,0:T(8,128)(2,1)}, u32[]{:S(2)}, u32[]{:S(2)}) collective-permute-start(bf16[512,768]{1,0:T(8,128)(2,1)} %get-tuple-element.41), channel_id=1, source_target_pairs={{0,4},{4,8},{8,12},{12,16},{16,20},{20,24},{24,28},{1,5},{5,9},{9,... | collective-permute-start | bytes 2359304 | tf_op jit(solution)/shard_map/ppermute | solution.py:20
  127.5 5.3 %collective-permute-start.3 = (bf16[512,768]{1,0:T(8,128)(2,1)}, bf16[512,768]{1,0:T(8,128)(2,1)}, u32[]{:S(2)}, u32[]{:S(2)}) collective-permute-start(bf16[512,768]{1,0:T(8,128)(2,1)} %get-tuple-element.38), channel_id=1, source_target_pairs={{4,0},{8,4},{12,8},{16,12},{20,16},{24,20},{28,24},{5,1},{9,5},{13... | collective-permute-start | bytes 2359304 | tf_op jit(solution)/shard_map/ppermute | solution.py:20
  128.8 5.3 %collective-permute-start.2 = (bf16[512,768]{1,0:T(8,128)(2,1)}, bf16[512,768]{1,0:T(8,128)(2,1)}, u32[]{:S(2)}, u32[]{:S(2)}) collective-permute-start(bf16[512,768]{1,0:T(8,128)(2,1)} %get-tuple-element.39), channel_id=1, source_target_pairs={{0,4},{4,8},{8,12},{12,16},{16,20},{20,24},{24,28},{1,5},{5,9},{9,... | collective-permute-start | bytes 2359304 | tf_op jit(solution)/shard_map/ppermute | solution.py:20
  134.1 1.4 copy-start.2
  135.5 104.0 %copy-start.7 = (bf16[1024,3072]{1,0:T(8,128)(2,1)S(1)}, bf16[1024,3072]{1,0:T(8,128)(2,1)}, u32[]{:S(2)}) copy-start(bf16[1024,3072]{1,0:T(8,128)(2,1)} %get-tuple-element.24) | copy-start | bytes 18874372
  210.0 36.5 %collective-permute-start.4 = (bf16[512,768]{1,0:T(8,128)(2,1)S(1)}, bf16[512,768]{1,0:T(8,128)(2,1)S(1)}, u32[]{:S(2)}, u32[]{:S(2)}) collective-permute-start(bf16[512,768]{1,0:T(8,128)(2,1)S(1)} %get-tuple-element.28), channel_id=1, source_target_pairs={{0,4},{4,8},{8,12},{12,16},{16,20},{20,24},{24,28},{1,5},{5,9},{9,... | collective-permute-start | bytes 2359304 | tf_op jit(solution)/shard_map/ppermute | solution.py:20
  234.8 11.7 %collective-permute-start.5 = (bf16[512,768]{1,0:T(8,128)(2,1)S(1)}, bf16[512,768]{1,0:T(8,128)(2,1)S(1)}, u32[]{:S(2)}, u32[]{:S(2)}) collective-permute-start(bf16[512,768]{1,0:T(8,128)(2,1)S(1)} %get-tuple-element.29), channel_id=1, source_target_pairs={{0,4},{4,8},{8,12},{12,16},{16,20},{20,24},{24,28},{1,5},{5,9},{9,... | collective-permute-start | bytes 2359304 | tf_op jit(solution)/shard_map/ppermute | solution.py:20
  236.7 9.8 %collective-permute-start.6 = (bf16[512,768]{1,0:T(8,128)(2,1)S(1)}, bf16[512,768]{1,0:T(8,128)(2,1)S(1)}, u32[]{:S(2)}, u32[]{:S(2)}) collective-permute-start(bf16[512,768]{1,0:T(8,128)(2,1)S(1)} %get-tuple-element.30), channel_id=1, source_target_pairs={{4,0},{8,4},{12,8},{16,12},{20,16},{24,20},{28,24},{5,1},{9,5},{13... | collective-permute-start | bytes 2359304 | tf_op jit(solution)/shard_map/ppermute | solution.py:20
  238.0 8.5 %collective-permute-start.7 = (bf16[512,768]{1,0:T(8,128)(2,1)S(1)}, bf16[512,768]{1,0:T(8,128)(2,1)S(1)}, u32[]{:S(2)}, u32[]{:S(2)}) collective-permute-start(bf16[512,768]{1,0:T(8,128)(2,1)S(1)} %get-tuple-element.31), channel_id=1, source_target_pairs={{4,0},{8,4},{12,8},{16,12},{20,16},{24,20},{28,24},{5,1},{9,5},{13... | collective-permute-start | bytes 2359304 | tf_op jit(solution)/shard_map/ppermute | solution.py:20
  246.4 0.9 copy-start.3
  246.4 1.2 copy-start.4
  246.5 1.4 copy-start.5
  246.5 1.6 copy-start.6
  256.5 7.9 %copy-start.8 = (bf16[1024,768]{1,0:T(8,128)(2,1)S(1)}, bf16[1024,768]{1,0:T(8,128)(2,1)}, u32[]{:S(2)}) copy-start(bf16[1024,768]{1,0:T(8,128)(2,1)} %get-tuple-element.34) | copy-start | bytes 4718596
  256.5 17.7 %slice-start = ((s8[4718592]{0:T(1024)(128)(4,1)}), s8[4194304]{0:T(1024)(128)(4,1)S(1)}, s32[]{:S(2)}) async-start(s8[4718592]{0:T(1024)(128)(4,1)} %bitcast.12), calls=%async_computation | async-start | bytes 8388608
  264.4 9.8 %slice-start.1 = ((s8[4718592]{0:T(1024)(128)(4,1)}), s8[524288]{0:T(1024)(128)(4,1)S(1)}, s32[]{:S(2)}) async-start(s8[4718592]{0:T(1024)(128)(4,1)} %bitcast.12), calls=%async_computation.1 | async-start | bytes 1048576

commit v3 on v2

--- a/solution.py
+++ b/solution.py
@@ -67,7 +67,7 @@
 def attend_kernel(
     bias_ref, gain_ref, raw_ref, grad_ref, kp_ref, ko_ref, kn_ref, vp_ref, vo_ref, vn_ref,
     att_ref, qpart_ref, dk_ref, dv_ref, dkp_ref, dvp_ref, dkn_ref, dvn_ref,
-    kt, vt, score, prob_grad, weight, score_grad, dk_acc, dv_acc,
+    kt, vt, score, prob_grad, weight, dk_acc, dv_acc,
 ):
     half = kp_ref.shape[0]
     total = dk_acc.shape[0]
@@ -146,7 +146,7 @@
 def attend(bias, gain, raw, grad, kp, ko, kn, vp, vo, vn):
     rows, local = raw.shape
     heads, half = local // HEAD_DIM, rows // 2
-    block = min(256, rows)
+    block = min(512, rows)
     by_row = pl.BlockSpec((block, HEAD_DIM), lambda h, j: (j, h))
     own = pl.BlockSpec((rows, HEAD_DIM), lambda h, j: (0, h))
     edge = pl.BlockSpec((half, HEAD_DIM), lambda h, j: (0, h))
@@ -170,7 +170,6 @@
             pltpu.VMEM((HEAD_DIM, window), jnp.bfloat16),
             pltpu.VMEM((window, block), jnp.float32),
             pltpu.VMEM((window, block), jnp.float32),
-            pltpu.VMEM((window, block), jnp.bfloat16),
             pltpu.VMEM((window, block), jnp.bfloat16),
             pltpu.VMEM((window, HEAD_DIM), jnp.float32),
             pltpu.VMEM((window, HEAD_DIM), jnp.float32),

time: 368 us -> 355 us (0.965)
  Pallas kernels: 292 us -> 280 us
    pallas_call x1, Pallas kernels: 74.5 us -> 61.8 us  [attend(): pl.pallas_call(attend_kernel, grid=(heads, rows // block), in_specs=[pl.B...]
where the time goes in v3:
time: 355 us
  Pallas kernels  280 us (79%)
  starting transfers between devices  39.9 us (11%)
  matrix products  24.6 us (7%)
  local copies, waits for them, and re-layouts  6.24 us (2%)
    pallas_call x1, Pallas kernels, project(): pl.pallas_call(functools.partial(project_kernel, count), in_specs=[vmem,...  118 us
    pallas_call x1, Pallas kernels, summed_over_frames(): pl.pallas_call(functools.partial(summed_kernel, count, number), in_specs=...  91.1 us
    pallas_call x1, Pallas kernels, attend(): pl.pallas_call(attend_kernel, grid=(heads, rows // block), in_specs=[pl.B...  61.8 us
    ppermute x8, starting transfers between devices, ppermute_by(): lax.ppermute(value, axis, [(source, source + steps) for source in range(i...  39.9 us
    dot_general x3, matrix products, weight_term(): lax.dot_general(gathered, grads, (((0,), (0,)), ((), ())), preferred_elem...  24.6 us
    pallas_call x1, Pallas kernels, key_back(): pl.pallas_call(key_back_kernel, grid=(local // HEAD_DIM,), in_specs=[spec...  8.38 us
  transfers between devices with their start and end apart: 8, of which 1 were waited for; matrix products, arithmetic and copies ran while one was open for 2% of the time, Pallas kernels for 0%

profile of v3, /device:TPU:0, one launch (start us, length us, event | category | flops | bytes accessed | tf_op | source)
XLA Modules:
  0.0 354.7 jit_solution(6908626340285305441)
XLA Ops:
  0.6 0.0 copy-start
  0.6 0.7 copy-done
  1.3 118.4 %project.1 = (bf16[1024,3072]{1,0:T(8,128)(2,1)}, f32[1024,768]{1,0:T(8,128)}, f32[1024,768]{1,0:T(8,128)}, bf16[1024,768]{1,0:T(8,128)(2,1)S(1)}, bf16[1024,768]{1,0:T(8,128)(2,1)S(1)}) custom-call(f32[2,128]{1,0:T(2,128)S(1)} %copy-done, bf16[256,3072]{1,0:T(8,128)(2,1)} %hidden_ref.1, bf16[3,3072,768]{2,1,0:T(8,128)(2,1)} %bitcast.17), custom_call_target="tpu_custom_call" | custom-call | tf_op jit(solution)/shard_map/project/pallas_call | solution.py:388
  119.8 0.0 copy-start.1
  119.8 1.2 fusion.1
  121.0 1.3 collective-permute-start.1
  122.3 3.9 %collective-permute-start = (bf16[512,768]{1,0:T(8,128)(2,1)}, bf16[512,768]{1,0:T(8,128)(2,1)}, u32[]{:S(2)}, u32[]{:S(2)}) collective-permute-start(bf16[512,768]{1,0:T(8,128)(2,1)} %get-tuple-element.41), channel_id=1, source_target_pairs={{0,4},{4,8},{8,12},{12,16},{16,20},{20,24},{24,28},{1,5},{5,9},{9,... | collective-permute-start | bytes 2359304 | tf_op jit(solution)/shard_map/ppermute | solution.py:20
  126.2 1.3 fusion
  127.5 1.3 collective-permute-start.3
  128.8 4.0 %collective-permute-start.2 = (bf16[512,768]{1,0:T(8,128)(2,1)}, bf16[512,768]{1,0:T(8,128)(2,1)}, u32[]{:S(2)}, u32[]{:S(2)}) collective-permute-start(bf16[512,768]{1,0:T(8,128)(2,1)} %get-tuple-element.39), channel_id=1, source_target_pairs={{0,4},{4,8},{8,12},{12,16},{16,20},{20,24},{24,28},{1,5},{5,9},{9,... | collective-permute-start | bytes 2359304 | tf_op jit(solution)/shard_map/ppermute | solution.py:20
  132.8 0.1 pad_maximum_fusion.1.bias_ref
  132.8 0.0 collective-permute-done.1.kn_ref
  132.8 0.0 collective-permute-done.kp_ref
  132.8 0.0 collective-permute-done.3.vn_ref
  132.8 1.2 collective-permute-done.2.vp_ref
  134.1 0.0 copy-done.1
  134.1 0.0 copy-start.2
  134.1 1.4 copy-done.2
  135.5 0.0 copy-start.7
  135.5 61.8 %attend.1 = (bf16[1024,768]{1,0:T(8,128)(2,1)}, bf16[1024,768]{1,0:T(8,128)(2,1)S(1)}, f32[1024,768]{1,0:T(8,128)}, f32[1024,768]{1,0:T(8,128)}, bf16[512,768]{1...) custom-call(f32[2]{0:T(128)S(1)} %pad_maximum_fusion.1.bias_ref, ...), custom_call_target="tpu_custom_call" | custom-call | flops 19327352832 | bytes 12582912 | tf_op jit(solution)/shard_map/attend/pallas_call | solution.py:158
  197.3 24.8 %collective-permute-start.4 = (bf16[512,768]{1,0:T(8,128)(2,1)S(1)}, bf16[512,768]{1,0:T(8,128)(2,1)S(1)}, u32[]{:S(2)}, u32[]{:S(2)}) collective-permute-start(bf16[512,768]{1,0:T(8,128)(2,1)S(1)} %get-tuple-element.28), channel_id=1, source_target_pairs={{0,4},{4,8},{8,12},{12,16},{16,20},{20,24},{24,28},{1,5},{5,9},{9,... | collective-permute-start | bytes 2359304 | tf_op jit(solution)/shard_map/ppermute | solution.py:20
  222.1 1.9 collective-permute-start.5
  224.0 1.3 collective-permute-start.6
  225.3 1.5 collective-permute-start.7
  226.8 0.0 copy-done.7
  226.8 6.9 %convolution_convert_fusion.2.refs_0_ = bf16[3072,768]{1,0:T(8,128)(2,1)} fusion(bf16[1024,3072]{1,0:T(8,128)(2,1)S(1)} %copy-done.7, bf16[1024,768]{1,0:T(8,128)(2,1)S(1)} %get-tuple-element.25), kind=kOutput, calls=%fused_computation.2 | convolution fusion | flops 4834197504 | bytes 12582912 | tf_op jit(solution)/shard_map/dot_general | solution.py:423
  233.7 0.0 collective-permute-done.4.pk_ref
  233.7 0.0 copy-start.3
  233.7 0.0 collective-permute-done.5.pv_ref
  233.7 0.0 copy-start.4
  233.8 0.0 collective-permute-done.6.nk_ref
  233.8 0.0 copy-start.5
  233.8 0.0 collective-permute-done.7.nv_ref
  233.8 0.0 copy-start.6
  233.8 0.8 copy-done.3
  234.6 0.3 copy-done.4
  234.9 0.2 copy-done.5
  235.1 0.3 copy-done.6
  235.4 8.4 %key_back.1 = (bf16[1024,768]{1,0:T(8,128)(2,1)}, bf16[1024,768]{1,0:T(8,128)(2,1)}) custom-call(f32[1024,768]{1,0:T(8,128)} %get-tuple-element.26.dk_ref, f32[1024,768]{1,0:T(8,128)} %get-tuple-element.27.dv_ref, bf16[512,768]{1,0:T(8,128)(2,1)} %copy-done.3, bf16[512,768]{1,0:T(8,128)(2,1)} %copy-done.4, bf16[512,768]{1,0:T(8,128)(2,1)} %copy-done.5, ...), custom_call_target="tpu_custom_call" | custom-call | tf_op jit(solution)/shard_map/key_back/pallas_call | solution.py:57
  243.8 0.0 slice-start
  243.8 7.9 %convolution_convert_fusion.1.refs_1_ = bf16[3072,768]{1,0:T(8,128)(2,1)S(1)} fusion(bf16[1024,3072]{1,0:T(8,128)(2,1)} %get-tuple-element.24, bf16[1024,768]{1,0:T(8,128)(2,1)} %get-tuple-element.33), kind=kOutput, calls=%fused_computation.1 | convolution fusion | flops 4834197504 | bytes 12582912 | tf_op jit(solution)/shard_map/dot_general | solution.py:423
  251.7 0.0 slice-start.1
  251.7 0.0 copy-done.8
  251.7 9.8 %convolution_convert_fusion.refs_2_ = bf16[3072,768]{1,0:T(8,128)(2,1)} fusion(bf16[1024,3072]{1,0:T(8,128)(2,1)} %get-tuple-element.24, bf16[1024,768]{1,0:T(8,128)(2,1)S(1)} %copy-done.8), kind=kOutput, calls=%fused_computation | convolution fusion | flops 4834197504 | bytes 12582912 | tf_op jit(solution)/shard_map/dot_general | solution.py:423
  261.5 0.0 slice-done
  261.5 0.0 slice-done.1
  261.5 91.1 %summed.1 = (f32[384,768]{1,0:T(8,128)S(1)}, f32[384,768]{1,0:T(8,128)S(1)}, f32[384,768]{1,0:T(8,128)S(1)}) custom-call(bf16[3072,768]{1,0:T(8,128)(2,1)S(1)} %bitcast.13, bf16[3072,768]{1,0:T(8,128)(2,1)S(1)} %convolution_convert_fusion.1.refs_1_, bf16[3072,768]{1,0:T(8,128)(2,1)} %convolution_convert_fusion.refs_2_), custom_call_target="tpu_custom_call" | custom-call | tf_op jit(solution)/shard_map/summed/pallas_call | solution.py:277
  352.6 2.0 pad_maximum_fusion
  (2 shorter events, 0.0 us)
Async XLA Ops:
  0.6 0.7 copy-start
  119.8 14.3 %copy-start.1 = (f32[2,128]{1,0:T(2,128)S(1)}, f32[2,128]{1,0:T(2,128)}, u32[]{:S(2)}) copy-start(f32[2,128]{1,0:T(2,128)} %gain_ref.5) | copy-start | bytes 3076
  121.0 11.8 %collective-permute-start.1 = (bf16[512,768]{1,0:T(8,128)(2,1)}, bf16[512,768]{1,0:T(8,128)(2,1)}, u32[]{:S(2)}, u32[]{:S(2)}) collective-permute-start(bf16[512,768]{1,0:T(8,128)(2,1)} %get-tuple-element.40), channel_id=1, source_target_pairs={{4,0},{8,4},{12,8},{16,12},{20,16},{24,20},{28,24},{5,1},{9,5},{13... | collective-permute-start | bytes 2359304 | tf_op jit(solution)/shard_map/ppermute | solution.py:20
  122.3 10.5 %collective-permute-start = (bf16[512,768]{1,0:T(8,128)(2,1)}, bf16[512,768]{1,0:T(8,128)(2,1)}, u32[]{:S(2)}, u32[]{:S(2)}) collective-permute-start(bf16[512,768]{1,0:T(8,128)(2,1)} %get-tuple-element.41), channel_id=1, source_target_pairs={{0,4},{4,8},{8,12},{12,16},{16,20},{20,24},{24,28},{1,5},{5,9},{9,... | collective-permute-start | bytes 2359304 | tf_op jit(solution)/shard_map/ppermute | solution.py:20
  127.5 5.3 %collective-permute-start.3 = (bf16[512,768]{1,0:T(8,128)(2,1)}, bf16[512,768]{1,0:T(8,128)(2,1)}, u32[]{:S(2)}, u32[]{:S(2)}) collective-permute-start(bf16[512,768]{1,0:T(8,128)(2,1)} %get-tuple-element.38), channel_id=1, source_target_pairs={{4,0},{8,4},{12,8},{16,12},{20,16},{24,20},{28,24},{5,1},{9,5},{13... | collective-permute-start | bytes 2359304 | tf_op jit(solution)/shard_map/ppermute | solution.py:20
  128.8 5.3 %collective-permute-start.2 = (bf16[512,768]{1,0:T(8,128)(2,1)}, bf16[512,768]{1,0:T(8,128)(2,1)}, u32[]{:S(2)}, u32[]{:S(2)}) collective-permute-start(bf16[512,768]{1,0:T(8,128)(2,1)} %get-tuple-element.39), channel_id=1, source_target_pairs={{0,4},{4,8},{8,12},{12,16},{16,20},{20,24},{24,28},{1,5},{5,9},{9,... | collective-permute-start | bytes 2359304 | tf_op jit(solution)/shard_map/ppermute | solution.py:20
  134.1 1.4 copy-start.2
  135.5 91.3 %copy-start.7 = (bf16[1024,3072]{1,0:T(8,128)(2,1)S(1)}, bf16[1024,3072]{1,0:T(8,128)(2,1)}, u32[]{:S(2)}) copy-start(bf16[1024,3072]{1,0:T(8,128)(2,1)} %get-tuple-element.24) | copy-start | bytes 18874372
  197.3 36.5 %collective-permute-start.4 = (bf16[512,768]{1,0:T(8,128)(2,1)S(1)}, bf16[512,768]{1,0:T(8,128)(2,1)S(1)}, u32[]{:S(2)}, u32[]{:S(2)}) collective-permute-start(bf16[512,768]{1,0:T(8,128)(2,1)S(1)} %get-tuple-element.28), channel_id=1, source_target_pairs={{0,4},{4,8},{8,12},{12,16},{16,20},{20,24},{24,28},{1,5},{5,9},{9,... | collective-permute-start | bytes 2359304 | tf_op jit(solution)/shard_map/ppermute | solution.py:20
  222.1 11.7 %collective-permute-start.5 = (bf16[512,768]{1,0:T(8,128)(2,1)S(1)}, bf16[512,768]{1,0:T(8,128)(2,1)S(1)}, u32[]{:S(2)}, u32[]{:S(2)}) collective-permute-start(bf16[512,768]{1,0:T(8,128)(2,1)S(1)} %get-tuple-element.29), channel_id=1, source_target_pairs={{0,4},{4,8},{8,12},{12,16},{16,20},{20,24},{24,28},{1,5},{5,9},{9,... | collective-permute-start | bytes 2359304 | tf_op jit(solution)/shard_map/ppermute | solution.py:20
  224.0 9.8 %collective-permute-start.6 = (bf16[512,768]{1,0:T(8,128)(2,1)S(1)}, bf16[512,768]{1,0:T(8,128)(2,1)S(1)}, u32[]{:S(2)}, u32[]{:S(2)}) collective-permute-start(bf16[512,768]{1,0:T(8,128)(2,1)S(1)} %get-tuple-element.30), channel_id=1, source_target_pairs={{4,0},{8,4},{12,8},{16,12},{20,16},{24,20},{28,24},{5,1},{9,5},{13... | collective-permute-start | bytes 2359304 | tf_op jit(solution)/shard_map/ppermute | solution.py:20
  225.3 8.5 %collective-permute-start.7 = (bf16[512,768]{1,0:T(8,128)(2,1)S(1)}, bf16[512,768]{1,0:T(8,128)(2,1)S(1)}, u32[]{:S(2)}, u32[]{:S(2)}) collective-permute-start(bf16[512,768]{1,0:T(8,128)(2,1)S(1)} %get-tuple-element.31), channel_id=1, source_target_pairs={{4,0},{8,4},{12,8},{16,12},{20,16},{24,20},{28,24},{5,1},{9,5},{13... | collective-permute-start | bytes 2359304 | tf_op jit(solution)/shard_map/ppermute | solution.py:20
  233.7 0.9 copy-start.3
  233.7 1.2 copy-start.4
  233.8 1.4 copy-start.5
  233.8 1.6 copy-start.6
  243.8 7.9 %copy-start.8 = (bf16[1024,768]{1,0:T(8,128)(2,1)S(1)}, bf16[1024,768]{1,0:T(8,128)(2,1)}, u32[]{:S(2)}) copy-start(bf16[1024,768]{1,0:T(8,128)(2,1)} %get-tuple-element.34) | copy-start | bytes 4718596
  243.8 17.7 %slice-start = ((s8[4718592]{0:T(1024)(128)(4,1)}), s8[4194304]{0:T(1024)(128)(4,1)S(1)}, s32[]{:S(2)}) async-start(s8[4718592]{0:T(1024)(128)(4,1)} %bitcast.12), calls=%async_computation | async-start | bytes 8388608
  251.7 9.8 %slice-start.1 = ((s8[4718592]{0:T(1024)(128)(4,1)}), s8[524288]{0:T(1024)(128)(4,1)S(1)}, s32[]{:S(2)}) async-start(s8[4718592]{0:T(1024)(128)(4,1)} %bitcast.12), calls=%async_computation.1 | async-start | bytes 1048576
